TPU v7x, 256 devices: a whole 4x4x8 slice. The times are simulated.
256 devices in a mesh: box: 4 (over z_lo), tile: 64 (over z_hi, y, x, core).
Axes of the slice: x: 4, y: 4, z: 8 (z_hi: 2, z_lo: 4; z = z_hi * 4 + z_lo), core: 2. Of those that a mesh axis runs over, the one named last changes fastest.
Arguments:
- box_maps: float32 [4, 6, 448, 2688], P('box', None, 'tile'), may hold values from -4.01 to 4.01, as said below
- face_slots: int32 [4, 6], replicated, may hold values from 0 to 5, each once within a row
Outputs:
- final_map: float32 [7168, 7168], P('tile', 'box')
Inputs may be any that keep to these rules, and one draw needn't show every extreme that they name: `box_maps`: read as a matrix of order 6 * 448 with rows and columns ordered by stored block and node, each box's map is exactly symmetric and positive definite. `face_slots`: each row is a permutation of the six stored blocks.
All inputs are finite; a program needn't handle non-finite values.
Results may differ from a plain program's by a relative error of at most 0.0001.
Values sent between devices are 32-bit elements; how exact they have to be, the bound alone decides.
No kernel may reach another device: no remote copies, remote signals or barrier semaphores. Data moves between devices by JAX's collectives and lax.ppermute only.
A program may use at most 64 MiB of HBM per device.

v0:
```python
import jax
import jax.numpy as jnp
from jax import lax
from jax.sharding import PartitionSpec as P

F = 448


def partner(value, axis, bit):
    mask = 2**bit
    pairs = [(source, source ^ mask) for source in range(lax.axis_size(axis))]
    return lax.ppermute(value, axis, pairs)


def copy_for_each(value, axis):
    copies = jnp.broadcast_to(value, (lax.axis_size(axis), *value.shape))
    return lax.all_to_all(copies, axis, split_axis=0, concat_axis=0, tiled=True)


def joined_along(parts, dim):
    parts = jnp.moveaxis(parts, 0, dim)
    shape = parts.shape
    return parts.reshape(*shape[:dim], shape[dim] * shape[dim + 1], *shape[dim + 2 :])


def gather_directly(value, axis, dim):
    parts = copy_for_each(value, axis)
    return joined_along(parts, dim)


def matmul(left, right):
    return jnp.dot(left, right, precision=lax.Precision.HIGHEST, preferred_element_type=jnp.float32)


def lower_solve(factor, coupled):
    return jax.scipy.linalg.solve_triangular(factor, coupled.T, lower=True).T


def face_columns(stored, slot_id):
    return lax.dynamic_slice_in_dim(stored, slot_id * F, F, stored.ndim - 1)


def beside(block_part, leading):
    empty_part = jnp.zeros_like(block_part)
    return jnp.where(
        leading,
        jnp.concatenate([block_part, empty_part], -1),
        jnp.concatenate([empty_part, block_part], -1),
    )


def ordered(own_piece, theirs, leading, axis_id):
    return jnp.where(
        leading,
        jnp.concatenate([own_piece, theirs], axis_id),
        jnp.concatenate([theirs, own_piece], axis_id),
    )


def per_device(box_maps, face_slots):
    stored = box_maps[0]
    node_count = stored.shape[1]
    box_id = lax.axis_index("box")
    along_x = box_id % 2
    along_y = box_id // 2
    leading = along_x == 0
    slot_row = lax.dynamic_index_in_dim(face_slots, box_id, 0, keepdims=False)

    def slot_of(surface):
        return lax.dynamic_index_in_dim(slot_row, surface, 0, keepdims=False)

    x_shared = slot_of(1 - along_x)
    y_shared = slot_of(3 - along_y)
    finals = [slot_of(along_x), slot_of(2 + along_y), slot_row[4], slot_row[5]]
    outer_rows = jnp.stack(
        [
            lax.dynamic_index_in_dim(stored, slot_id, 0, keepdims=False)
            for slot_id in finals + [y_shared]
        ]
    )
    shared_face = lax.dynamic_index_in_dim(stored, x_shared, 0, keepdims=False)
    own_part = face_columns(shared_face, x_shared)
    summed = own_part + partner(own_part, "box", 0)
    factor = jnp.linalg.cholesky(gather_directly(summed, "tile", 0))
    level_one = lower_solve(
        factor, face_columns(outer_rows, x_shared).reshape(5 * node_count, F)
    ).reshape(5, node_count, F)
    final_one = level_one[:4].reshape(4 * node_count, F)
    pairing_rows = level_one[4]
    partner_rows = partner(pairing_rows, "box", 0)
    pair_rows = gather_directly(
        ordered(pairing_rows[None], partner_rows[None], leading, 0), "tile", 1
    ).reshape(2 * F, F)
    partial_rows = beside(face_columns(outer_rows[4], y_shared), leading) - matmul(
        pairing_rows, pair_rows.T
    )
    summed_rows = partial_rows + partner(partial_rows, "box", 1)
    half_rows = gather_directly(summed_rows, "tile", 0)
    shared_two = ordered(half_rows, partner(half_rows, "box", 0), leading, 0)
    factor_two = jnp.linalg.cholesky(shared_two)
    coupled = beside(face_columns(outer_rows[:4], y_shared), leading).reshape(
        4 * node_count, 2 * F
    ) - matmul(final_one, pair_rows.T)
    level_two = lower_solve(factor_two, coupled)
    coupling_rows = jnp.concatenate([final_one, level_two], 1).reshape(4, node_count, 3 * F)
    own_block = jnp.concatenate([face_columns(outer_rows[:4], slot_id) for slot_id in finals], 2)
    tile_count = lax.axis_size("tile")
    tile_bits = tile_count.bit_length() - 1
    column_bits = (tile_bits + 2) // 2
    columns = 1 << column_bits
    high_count = tile_count >> column_bits
    tile_id = lax.axis_index("tile")
    row_panel = coupling_rows
    for bit_id in range(column_bits):
        lower_half = (tile_id >> bit_id) % 2 == 0
        row_panel = ordered(row_panel, partner(row_panel, "tile", bit_id), lower_half, 1)
    group_rows = 4 * columns * node_count
    row_panel = row_panel.reshape(group_rows, 3 * F)
    column_rows = coupling_rows[:, None]
    column_own = own_block[:, None]
    for bit_id in range(column_bits, tile_bits):
        lower_half = (tile_id >> bit_id) % 2 == 0
        their_rows, their_own = partner((column_rows, column_own), "tile", bit_id)
        column_rows = ordered(column_rows, their_rows, lower_half, 1)
        column_own = ordered(column_own, their_own, lower_half, 1)
    column_rows = lax.all_gather(column_rows, "box", axis=0, tiled=True).reshape(
        16 * high_count * node_count, 3 * F
    )
    box_span = 4 * high_count * node_count
    pair_id = box_id // 2
    pair_cols = lax.dynamic_slice_in_dim(column_rows, pair_id * 2 * box_span, 2 * box_span, 0)[
        :, :F
    ]
    pair_term = matmul(row_panel[:, :F], pair_cols.T)
    group_id = tile_id >> column_bits
    mirrored = lax.dynamic_slice_in_dim(
        column_own.reshape(4, high_count, node_count, 4, F),
        group_id * columns * node_count,
        columns * node_count,
        4,
    )
    own_term = mirrored.transpose(3, 4, 0, 1, 2).reshape(group_rows, box_span)
    own_cols = lax.dynamic_slice_in_dim(pair_term, along_x * box_span, box_span, 1)
    pair_block = lax.dynamic_update_slice_in_dim(
        -pair_term, own_term - own_cols, along_x * box_span, 1
    )
    level_block = lax.dynamic_update_slice_in_dim(
        jnp.zeros((group_rows, 4 * box_span), jnp.float32), pair_block, pair_id * 2 * box_span, 1
    )
    level_block = level_block - matmul(row_panel[:, F:], column_rows[:, F:].T)
    piece_width = 16 * node_count // columns
    outgoing = level_block.reshape(group_rows, tile_count, piece_width)
    incoming = lax.all_to_all(outgoing, "tile", split_axis=1, concat_axis=1, tiled=True)
    incoming = incoming.reshape(
        4, columns * node_count, high_count, columns, 16 // columns, node_count
    )
    return incoming.transpose(4, 3, 5, 0, 2, 1).reshape(16 * node_count, 4 * F)


def solution(mesh):
    return jax.shard_map(
        per_device,
        mesh=mesh,
        in_specs=(P("box", None, "tile", None), P()),
        out_specs=P("tile", "box"),
        check_vma=False,
    )
```

profile of v0, /device:TPU:33, one launch (start us, length us, event | category | flops | bytes accessed | tf_op | source)
XLA Modules:
  0.0 830.7 jit_solution(5303015322227357622)
XLA Ops:
  17.8 15.0 %all-to-all-start = ((f32[64,7,448]{2,1,0:T(8,128)}), f32[64,7,448]{2,1,0:T(8,128)S(1)}, u32[]{:S(2)}, u32[]{:S(2)}) async-start(f32[64,7,448]{2,1,0:T(8,128)} %broadcast_in_dim.25), calls=%async_computation | async-start | bytes 2097152 | tf_op jit(solution)/shard_map/all_to_all | solution.py:17
  43.5 21.4 %all-to-all-done = f32[64,7,448]{2,1,0:T(8,128)S(1)} async-done(((f32[64,7,448]{2,1,0:T(8,128)}), f32[64,7,448]{2,1,0:T(8,128)S(1)}, u32[]{:S(2)}, u32[]{:S(2)}) %all-to-all-start) | async-done | bytes 802848 | tf_op jit(solution)/shard_map/all_to_all | solution.py:17
  65.5 11.7 %cholesky.294 = f32[128,128]{1,0:T(8,128)S(1)} custom-call(f32[128,128]{1,0:T(8,128)S(1)} %cholesky.762), custom_call_target="Cholesky" | custom-call | tf_op jit(solution)/shard_map/jit(cholesky)/cholesky | solution.py:84
  87.8 11.7 %cholesky.317 = f32[128,128]{1,0:T(8,128)S(1)} custom-call(f32[128,128]{1,0:T(8,128)S(1)} %cholesky.766), custom_call_target="Cholesky" | custom-call | tf_op jit(solution)/shard_map/jit(cholesky)/cholesky | solution.py:84
  110.1 11.7 %cholesky.342 = f32[128,128]{1,0:T(8,128)S(1)} custom-call(f32[128,128]{1,0:T(8,128)S(1)} %cholesky.771), custom_call_target="Cholesky" | custom-call | tf_op jit(solution)/shard_map/jit(cholesky)/cholesky | solution.py:84
  148.8 39.5 %custom-call.89 = f32[4,128,128]{1,2,0:T(8,128)S(1)} custom-call(f32[4,128,128]{2,1,0:T(8,128)S(1)} %pad_maximum_fusion.3), custom_call_target="InvertDiagBlocksLowerTriangular" | custom-call | tf_op jit(solution)/shard_map/jit(_solve_triangular)/triangular_solve | solution.py:36
  200.7 48.1 %all-to-all-done.1 = f32[64,2,7,448]{3,1,2,0:T(2,128)S(1)} async-done(((f32[64,2,7,448]{3,1,2,0:T(2,128)}), f32[64,2,7,448]{3,1,2,0:T(2,128)S(1)}, u32[]{:S(2)}, u32[]{:S(2)}) %all-to-all-start.1) | async-done | bytes 1605664 | tf_op jit(solution)/shard_map/all_to_all | solution.py:17
  257.5 54.5 %all_to_all.20 = f32[64,7,896]{2,1,0:T(8,128)} all-to-all(f32[64,7,896]{2,1,0:T(8,128)S(1)} %broadcast_in_dim.28), channel_id=1, replica_groups=mesh['box'=4,'tile'=64] {'tile'}, dimensions={0} | all-to-all | bytes 3211264 | tf_op jit(solution)/shard_map/all_to_all | solution.py:17
  326.4 23.9 %collective-permute-done.3 = f32[448,896]{1,0:T(8,128)} collective-permute-done((f32[448,896]{1,0:T(8,128)S(1)}, f32[448,896]{1,0:T(8,128)}, u32[]{:S(2)}, u32[]{:S(2)}) %collective-permute-start.3) | collective-permute-done | bytes 1605664 | tf_op jit(solution)/shard_map/ppermute | solution.py:12
  364.8 11.7 %cholesky.635 = f32[128,128]{1,0:T(8,128)S(1)} custom-call(f32[128,128]{1,0:T(8,128)S(1)} %cholesky.775), custom_call_target="Cholesky" | custom-call | tf_op jit(solution)/shard_map/jit(cholesky)/cholesky | solution.py:100
  390.3 11.7 %cholesky.650 = f32[128,128]{1,0:T(8,128)S(1)} custom-call(f32[128,128]{1,0:T(8,128)S(1)} %cholesky.779), custom_call_target="Cholesky" | custom-call | tf_op jit(solution)/shard_map/jit(cholesky)/cholesky | solution.py:100
  415.7 13.2 %cholesky.671 = f32[128,128]{1,0:T(8,128)} custom-call(f32[128,128]{1,0:T(8,128)} %cholesky.784), custom_call_target="Cholesky" | custom-call | tf_op jit(solution)/shard_map/jit(cholesky)/cholesky | solution.py:100
  430.3 11.3 %custom-call.92 = f32[1,128,128]{1,2,0:T(8,128)} custom-call(f32[1,128,128]{2,1,0:T(8,128)} %get-tuple-element.69), custom_call_target="InvertDiagBlocksLowerTriangular" | custom-call | tf_op jit(solution)/shard_map/jit(cholesky)/cholesky | solution.py:100
  445.2 12.7 %cholesky.690 = f32[128,128]{1,0:T(8,128)S(1)} custom-call(f32[128,128]{1,0:T(8,128)} %cholesky.789), custom_call_target="Cholesky" | custom-call | tf_op jit(solution)/shard_map/jit(cholesky)/cholesky | solution.py:100
  471.3 11.7 %cholesky.709 = f32[128,128]{1,0:T(8,128)S(1)} custom-call(f32[128,128]{1,0:T(8,128)S(1)} %cholesky.794), custom_call_target="Cholesky" | custom-call | tf_op jit(solution)/shard_map/jit(cholesky)/cholesky | solution.py:100
  495.3 12.1 %cholesky.729 = f32[128,128]{1,0:T(8,128)S(1)} custom-call(f32[128,128]{1,0:T(8,128)S(1)} %cholesky.799), custom_call_target="Cholesky" | custom-call | tf_op jit(solution)/shard_map/jit(cholesky)/cholesky | solution.py:100
  518.8 11.7 %cholesky.747 = f32[128,128]{1,0:T(8,128)S(1)} custom-call(f32[128,128]{1,0:T(8,128)S(1)} %slice_subtract_fusion.5), custom_call_target="Cholesky" | custom-call | tf_op jit(solution)/shard_map/jit(cholesky)/cholesky | solution.py:100
  542.2 24.5 %while.3 = (s32[]{:T(128)}, f32[896,896]{1,0:T(8,128)}, s32[7,2]{0,1:T(2,128)S(1)}, f32[7,128,128]{2,1,0:T(8,128)}, s32[]{:T(128)}) while((s32[]{:T(128)}, f32[896,896]{1,0:T(8,128)}, s32[7,2]{0,1:T(2,128)S(1)}, f32[7,128,128]{2,1,0:T(8,128)}, s32[]{:T(128)}) %tuple.88), condition=%wide.while_cond.1, body=%wide.while_body.1.sunk | while | flops 2 | bytes 132205 | solution.py:36
  566.8 69.7 %custom-call.96 = f32[7,128,128]{1,2,0:T(8,128)S(1)} custom-call(f32[7,128,128]{2,1,0:T(8,128)} %get-tuple-element.20), custom_call_target="InvertDiagBlocksLowerTriangular" | custom-call | tf_op jit(solution)/shard_map/jit(_solve_triangular)/triangular_solve | solution.py:36
  652.8 21.0 %collective-permute-done.9 = f32[4,2,7,1344]{3,2,0,1:T(8,128)S(1)} collective-permute-done((f32[4,2,7,1344]{3,2,0,1:T(8,128)S(1)}, f32[4,2,7,1344]{3,2,0,1:T(8,128)S(1)}, u32[]{:S(2)}, u32[]{:S(2)}) %collective-permute-start.9) | collective-permute-done | bytes 301088 | tf_op jit(solution)/shard_map/ppermute | solution.py:12
  688.5 14.6 %collective-permute-done.6 = f32[4,28,1344]{2,0,1:T(4,128)S(1)} collective-permute-done((f32[4,28,1344]{2,0,1:T(4,128)S(1)}, f32[4,28,1344]{2,0,1:T(4,128)S(1)}, u32[]{:S(2)}, u32[]{:S(2)}) %collective-permute-start.6) | collective-permute-done | bytes 602144 | tf_op jit(solution)/shard_map/ppermute | solution.py:12
  706.6 29.7 %collective-permute-done.10 = f32[4,1,7,1792]{3,0,2,1:T(4,128)S(1)} collective-permute-done((f32[4,1,7,1792]{3,0,2,1:T(4,128)S(1)}, f32[4,1,7,1792]{3,0,2,1:T(4,128)S(1)}, u32[]{:S(2)}, u32[]{:S(2)}) %collective-permute-start.10) | collective-permute-done | bytes 200736 | tf_op jit(solution)/shard_map/ppermute | solution.py:12
  737.8 21.8 %collective-permute-done.11 = f32[4,2,7,1792]{3,0,2,1:T(4,128)S(1)} collective-permute-done((f32[4,2,7,1792]{3,0,2,1:T(4,128)S(1)}, f32[4,2,7,1792]{3,0,2,1:T(4,128)S(1)}, u32[]{:S(2)}, u32[]{:S(2)}) %collective-permute-start.11) | collective-permute-done | bytes 401440 | tf_op jit(solution)/shard_map/ppermute | solution.py:12
  783.0 37.5 %all_to_all.21 = f32[448,64,7]{0,2,1:T(8,128)S(1)} all-to-all(f32[448,64,7]{0,2,1:T(8,128)S(1)} %reshape.188), channel_id=1, replica_groups=mesh['box'=4,'tile'=64] {'tile'}, dimensions={1} | all-to-all | bytes 1605632 | tf_op jit(solution)/shard_map/all_to_all | solution.py:153
  (251 shorter events, 271.5 us)
Async XLA Ops:
  6.5 35.5 %copy-start.9 = (f32[1,6,7,2688]{3,0,2,1:T(1,128)S(1)}, f32[1,6,7,2688]{3,0,2,1:T(1,128)}, u32[]{:S(2)}) copy-start(f32[1,6,7,2688]{3,0,2,1:T(1,128)} %param.2) | copy-start | bytes 1354756
  14.0 2.7 collective-permute-start
  17.8 47.0 %all-to-all-start = ((f32[64,7,448]{2,1,0:T(8,128)}), f32[64,7,448]{2,1,0:T(8,128)S(1)}, u32[]{:S(2)}, u32[]{:S(2)}) async-start(f32[64,7,448]{2,1,0:T(8,128)} %broadcast_in_dim.25), calls=%async_computation | async-start | bytes 2097152 | tf_op jit(solution)/shard_map/all_to_all | solution.py:17
  189.9 131.4 %copy-start.3 = (f32[35,448]{1,0:T(8,128)}, f32[35,448]{1,0:T(8,128)S(1)}, u32[]{:S(2)}) copy-start(f32[35,448]{1,0:T(8,128)S(1)} %maximum_bitcast_fusion) | copy-start | bytes 188164
  189.9 2.7 collective-permute-start.1
  194.4 54.4 %all-to-all-start.1 = ((f32[64,2,7,448]{3,1,2,0:T(2,128)}), f32[64,2,7,448]{3,1,2,0:T(2,128)S(1)}, u32[]{:S(2)}, u32[]{:S(2)}) async-start(f32[64,2,7,448]{3,1,2,0:T(2,128)} %broadcast_in_dim.27), calls=%async_computation.1 | async-start | bytes 3670016 | tf_op jit(solution)/shard_map/all_to_all | solution.py:17
  200.6 563.7 %all-gather.2.cloned.1.call-start = ((), (), s32[]{:S(2)}) async-start(), calls=%async_computation.4 | async-start | bytes 3604480 | tf_op jit(solution)/shard_map/all_gather | solution.py:126
  253.7 3.6 collective-permute-start.2
  313.6 36.7 %collective-permute-start.3 = (f32[448,896]{1,0:T(8,128)S(1)}, f32[448,896]{1,0:T(8,128)}, u32[]{:S(2)}, u32[]{:S(2)}) collective-permute-start(f32[448,896]{1,0:T(8,128)S(1)} %reshape.183), channel_id=1, source_target_pairs={{0,64},{64,0},{128,192},{192,128},{1,65},{65,1},{129,193},{193,129... | collective-permute-start | bytes 4816904 | tf_op jit(solution)/shard_map/ppermute | solution.py:12
  540.3 96.2 %copy-start.8 = (f32[896,28]{0,1:T(8,128)S(1)}, f32[896,28]{0,1:T(8,128)}, u32[]{:S(2)}) copy-start(f32[896,28]{0,1:T(8,128)} %fusion.9) | copy-start | bytes 301060
  542.2 103.2 %slice-start = ((f32[35,448]{1,0:T(8,128)}), f32[28,448]{1,0:T(8,128)S(1)}, s32[]{:S(2)}) async-start(f32[35,448]{1,0:T(8,128)} %copy-done.3), calls=%async_computation.5 | async-start | bytes 131072 | tf_op jit(solution)/shard_map/slice | solution.py:88
  645.6 6.6 collective-permute-start.8
  652.2 21.5 %collective-permute-start.9 = (f32[4,2,7,1344]{3,2,0,1:T(8,128)S(1)}, f32[4,2,7,1344]{3,2,0,1:T(8,128)S(1)}, u32[]{:S(2)}, u32[]{:S(2)}) collective-permute-start(f32[4,2,7,1344]{3,2,0,1:T(8,128)S(1)} %maximum_select_fusion.7), channel_id=1, source_target_pairs={{0,32},{1,33},{2,34},{3,35},{4,36},{5,37},{6,38},{7,39},{8,40},{9,... | collective-permute-start | bytes 903176 | tf_op jit(solution)/shard_map/ppermute | solution.py:12
  674.7 1.6 collective-permute-start.4
  676.5 9.8 %collective-permute-start.5 = (f32[4,14,1344]{2,1,0:T(8,128)S(1)}, f32[4,14,1344]{2,1,0:T(8,128)S(1)}, u32[]{:S(2)}, u32[]{:S(2)}) collective-permute-start(f32[4,14,1344]{2,1,0:T(8,128)S(1)} %maximum_select_fusion.6), channel_id=1, source_target_pairs={{0,2},{1,3},{2,0},{3,1},{4,6},{5,7},{6,4},{7,5},{8,10},{9,11},{10,... | collective-permute-start | bytes 903176 | tf_op jit(solution)/shard_map/ppermute | solution.py:12
  676.6 28.4 %copy-start.10 = (f32[4,7,448]{2,0,1:T(4,128)S(1)}, f32[4,7,448]{2,0,1:T(4,128)}, u32[]{:S(2)}) copy-start(f32[4,7,448]{2,0,1:T(4,128)} %get-tuple-element.50) | copy-start | bytes 150532
  676.6 28.4 %copy-start.11 = (f32[4,7,448]{2,0,1:T(4,128)S(1)}, f32[4,7,448]{2,0,1:T(4,128)}, u32[]{:S(2)}) copy-start(f32[4,7,448]{2,0,1:T(4,128)} %get-tuple-element.51) | copy-start | bytes 150532
  676.6 28.3 %copy-start.12 = (f32[4,7,448]{2,0,1:T(4,128)S(1)}, f32[4,7,448]{2,0,1:T(4,128)}, u32[]{:S(2)}) copy-start(f32[4,7,448]{2,0,1:T(4,128)} %get-tuple-element.52) | copy-start | bytes 150532
  676.6 28.3 %copy-start.13 = (f32[4,7,448]{2,0,1:T(4,128)S(1)}, f32[4,7,448]{2,0,1:T(4,128)}, u32[]{:S(2)}) copy-start(f32[4,7,448]{2,0,1:T(4,128)} %get-tuple-element.53) | copy-start | bytes 150532
  686.9 16.2 %collective-permute-start.6 = (f32[4,28,1344]{2,0,1:T(4,128)S(1)}, f32[4,28,1344]{2,0,1:T(4,128)S(1)}, u32[]{:S(2)}, u32[]{:S(2)}) collective-permute-start(f32[4,28,1344]{2,0,1:T(4,128)S(1)} %copy.87), channel_id=1, source_target_pairs={{0,4},{1,5},{2,6},{3,7},{4,0},{5,1},{6,2},{7,3},{8,12},{9,13},{10,... | collective-permute-start | bytes 1806344 | tf_op jit(solution)/shard_map/ppermute | solution.py:12
  703.3 57.5 %collective-permute-start.7 = (f32[4,56,1344]{2,1,0:T(8,128)S(1)}, f32[4,56,1344]{2,1,0:T(8,128)}, u32[]{:S(2)}, u32[]{:S(2)}) collective-permute-start(f32[4,56,1344]{2,1,0:T(8,128)S(1)} %maximum_select_fusion.2), channel_id=1, source_target_pairs={{0,8},{1,9},{2,10},{3,11},{4,12},{5,13},{6,14},{7,15},{8,0},{9,1},... | collective-permute-start | bytes 3612680 | tf_op jit(solution)/shard_map/ppermute | solution.py:12
  705.2 31.1 %collective-permute-start.10 = (f32[4,1,7,1792]{3,0,2,1:T(4,128)S(1)}, f32[4,1,7,1792]{3,0,2,1:T(4,128)S(1)}, u32[]{:S(2)}, u32[]{:S(2)}) collective-permute-start(f32[4,1,7,1792]{3,0,2,1:T(4,128)S(1)} %bitcast.198), channel_id=1, source_target_pairs={{0,16},{1,17},{2,18},{3,19},{4,20},{5,21},{6,22},{7,23},{8,24},{9,... | collective-permute-start | bytes 602120 | tf_op jit(solution)/shard_map/ppermute | solution.py:12
  736.3 23.3 %collective-permute-start.11 = (f32[4,2,7,1792]{3,0,2,1:T(4,128)S(1)}, f32[4,2,7,1792]{3,0,2,1:T(4,128)S(1)}, u32[]{:S(2)}, u32[]{:S(2)}) collective-permute-start(f32[4,2,7,1792]{3,0,2,1:T(4,128)S(1)} %maximum_select_fusion.5), channel_id=1, source_target_pairs={{0,32},{1,33},{2,34},{3,35},{4,36},{5,37},{6,38},{7,39},{8,40},{9,... | collective-permute-start | bytes 1204232 | tf_op jit(solution)/shard_map/ppermute | solution.py:12
  768.1 9.1 %copy-start = (f32[4,112,1344]{2,1,0:T(8,128)S(1)}, f32[4,112,1344]{2,1,0:T(8,128)}, u32[]{:S(2)}) copy-start(f32[4,112,1344]{2,1,0:T(8,128)} %maximum_select_fusion.1) | copy-start | bytes 7225348
  (7 other events, 9.9 us)
Sparse Core Ops, SparseCore 0:
  674.8 57.3 all-gather.1
where the time goes:
time: 835 us; the launch traced here: 831 us
  other arithmetic  353 us (42%)
  waiting for transfers between devices  204 us (24%)
  blocking collectives  92 us (11%)
  local copies, waits for them, and re-layouts  75.1 us (9%)
  matrix products  38.6 us (5%)
  between operations  37.2 us (4%)
  starting transfers between devices  30.5 us (4%)
    another operation x27, other arithmetic, per_device(): factor_two = jnp.linalg.cholesky(shared_two)  154 us
    ppermute x12, waiting for transfers between devices, partner(): return lax.ppermute(value, axis, pairs)  135 us
    another operation x10, other arithmetic, lower_solve(): return jax.scipy.linalg.solve_triangular(factor, coupled.T, lower=True).T  112 us
    another operation x14, other arithmetic, per_device(): factor = jnp.linalg.cholesky(gather_directly(summed, 'tile', 0))  72.7 us
    all_to_all x2, waiting for transfers between devices, copy_for_each(): return lax.all_to_all(copies, axis, split_axis=0, concat_axis=0, tiled=True)  69.5 us
    all_to_all x1, blocking collectives, copy_for_each(): return lax.all_to_all(copies, axis, split_axis=0, concat_axis=0, tiled=True)  54.5 us
    all_to_all x1, blocking collectives, per_device(): lax.all_to_all(outgoing, 'tile', split_axis=1, concat_axis=1, tiled=True)  37.5 us
    another operation x30, local copies, waits for them, and re-layouts  30.5 us
  transfers between devices with their start and end apart: 15, of which 13 were waited for; matrix products, arithmetic and copies ran while one was open for 2% of the time, Pallas kernels for 0%

commit v1 on v0

v1 whole, which is shorter than its diff:
```python
import functools

import jax
import jax.numpy as jnp
from jax import lax
from jax.experimental import pallas as pl
from jax.experimental.pallas import tpu as pltpu
from jax.sharding import PartitionSpec as P

F = 448
NODES = 7
LANES = 128
MICRO = 16
VMEM_BYTES = 56 * 1024 * 1024


def tile_of(z, y, x, core):
    return ((z * 4 + y) * 4 + x) * 2 + core


PLANES = [
    [tile_of(z, y, x, core) for y in range(4) for x in range(4)]
    for z in range(2)
    for core in range(2)
]
QUARTERS = [[16 * quarter + own for own in range(16)] for quarter in range(4)]


def matmul(left, right):
    return jnp.dot(left, right, precision=lax.Precision.HIGHEST, preferred_element_type=jnp.float32)


def matmul_nt(left, right):
    return lax.dot_general(
        left,
        right,
        (((1,), (1,)), ((), ())),
        precision=lax.Precision.HIGHEST,
        preferred_element_type=jnp.float32,
    )


def invert(stack):
    full = (8, LANES)
    lane = lax.broadcasted_iota(jnp.int32, full, 1)
    sub = lax.broadcasted_iota(jnp.int32, full, 0)

    def along_rows(value, row):
        return jnp.broadcast_to(value[row : row + 1, :], full)

    def along_lanes(value, column):
        return jnp.broadcast_to(value[:, column : column + 1], full)

    stack = [list(rows) for rows in stack]
    count = len(stack[0])
    which = range(len(stack))
    for start in range(0, 8 * count, MICRO):
        first = start // 8
        inside = (lane >= start) & (lane < start + MICRO)
        following = [group for group in (first + 2, first + 3) if group < count]
        rest = [g for g in range(count) if g not in (first, first + 1, *following)]
        pivots = [
            [[along_lanes(stack[n][first + h], start + k) for h in range(2)] for k in range(MICRO)]
            for n in which
        ]
        rows = [
            [
                jnp.where(
                    inside,
                    jnp.where(lane == start + 8 * h + sub, 1.0, 0.0),
                    stack[n][first + h],
                )
                for h in range(2)
            ]
            for n in which
        ]
        ahead = [
            [[along_lanes(stack[n][group], start + k) for k in range(MICRO)] for group in following]
            for n in which
        ]
        for j in range(MICRO):
            half, row = divmod(j, 8)
            chosen = sub == row
            for n in which:
                scale = 1.0 / along_rows(pivots[n][j][half], row)
                pivot_row = along_rows(rows[n][half], row) * scale
                for k in range(j + 1, MICRO):
                    scaled = along_rows(pivots[n][k][half], row) * scale
                    for h in range(2):
                        value = pivots[n][k][h] - pivots[n][j][h] * scaled
                        pivots[n][k][h] = jnp.where(chosen, scaled, value) if h == half else value
                for h in range(2):
                    value = rows[n][h] - pivots[n][j][h] * pivot_row
                    rows[n][h] = jnp.where(chosen, pivot_row, value) if h == half else value
        for n in which:
            spread = [along_rows(rows[n][k // 8], k % 8) for k in range(MICRO)]
            for position, group in enumerate(following):
                terms = [ahead[n][position][k] * spread[k] for k in range(MICRO)]
                while len(terms) > 1:
                    terms = [terms[i] + terms[i + 1] for i in range(0, len(terms), 2)]
                stack[n][group] = jnp.where(inside, 0.0, stack[n][group]) - terms[0]
            if rest:
                zero = jnp.zeros(full, jnp.float32)
                held = jnp.concatenate([stack[n][group] for group in rest], 0)
                panel = jnp.concatenate(
                    [zero] * first + rows[n] + [zero] * (LANES // 8 - first - 2), 0
                )
                update = matmul(held, panel)
                for i, group in enumerate(rest):
                    stack[n][group] = (
                        jnp.where(inside, 0.0, stack[n][group]) - update[8 * i : 8 * i + 8]
                    )
            stack[n][first], stack[n][first + 1] = rows[n]
    return stack


def groups_of(value):
    return [value[8 * g : 8 * g + 8, :] for g in range(value.shape[0] // 8)]


def node_orders(z, core):
    shape = (F, 256)
    target = lax.broadcasted_iota(jnp.int32, shape, 0)
    source = lax.broadcasted_iota(jnp.int32, shape, 1)
    inner = source % 8
    half = (source // 8) % 2
    place = source // 16
    half = jnp.where(z == 1, 1 - half, half)
    orders = []
    for held_core in (core, 1 - core):
        node = NODES * ((half * 16 + place) * 2 + held_core) + inner
        hit = (node == target) & (inner < NODES)
        orders.append(jnp.where(hit, 1.0, 0.0).astype(jnp.bfloat16))
    return orders


def in_node_order(orders, pieces):
    total = None
    for order, piece in zip(orders, pieces):
        for _ in range(3):
            part = piece.astype(jnp.bfloat16)
            piece = piece - part.astype(jnp.float32)
            term = jnp.dot(order, part, preferred_element_type=jnp.float32)
            total = term if total is None else total + term
    return total


def pair_kernel(place_ref, own_ref, other_ref, inverse_ref, work, panel):
    orders = node_orders(place_ref[0], place_ref[1])
    work[...] = jnp.zeros_like(work)
    for n in range(2):
        pieces = [ref[:, :, n].reshape(256, F) for ref in (own_ref, other_ref)]
        work[n, :F, :F] = in_node_order(orders, pieces)

    def eliminate(block, height):
        at = pl.ds(pl.multiple_of(block * LANES, LANES), LANES)
        squares = [groups_of(work[n, at, at])[: height // 8] for n in range(2)]
        inverses = invert(squares)
        for n in range(2):
            square = jnp.concatenate(inverses[n], 0)
            if height < LANES:
                square = jnp.concatenate(
                    [square, jnp.zeros((LANES - height, LANES), jnp.float32)], 0
                )
            panel[n] = matmul(square, work[n, at, :])
            panel[n, :, at] = square

        def update(step, carry):
            index = step + jnp.where(step >= block, 1, 0)
            rows = pl.ds(pl.multiple_of(index * LANES, LANES), LANES)
            for n in range(2):
                left = work[n, rows, at]
                work[n, rows, at] = jnp.zeros((LANES, LANES), jnp.float32)
                work[n, rows, :] = work[n, rows, :] - matmul(left, panel[n])
            return carry

        lax.fori_loop(0, 3, update, 0)
        for n in range(2):
            work[n, at, :] = panel[n]

    def step(block, carry):
        eliminate(block, LANES)
        return carry

    lax.fori_loop(0, 3, step, 0)
    eliminate(jnp.int32(3), F - 3 * LANES)
    inverse_ref[...] = work[:, :F, :F]


def merge_kernel(
    place_ref,
    own_ref,
    other_ref,
    inverse_ref,
    coupled_ref,
    direct_ref,
    first_ref,
    second_ref,
    coupling,
    weighted,
    system,
    panel,
):
    orders = node_orders(place_ref[0], place_ref[1])

    def ordered(index):
        pieces = [ref[:, :, index].reshape(256, 512) for ref in (own_ref, other_ref)]
        return in_node_order(orders, pieces)

    for pair in range(2):
        for side in range(2):
            coupling[pair, side * F : side * F + F, :] = ordered(2 * pair + side)[:, :F]

    def weigh(index, carry):
        rows = pl.ds(pl.multiple_of(index * LANES, LANES), LANES)
        for pair in range(2):
            weighted[pair, rows, :] = matmul(coupling[pair, rows, :], inverse_ref[pair])
        return carry

    lax.fori_loop(0, 7, weigh, 0)

    def build(index, carry):
        rows = pl.ds(pl.multiple_of(index * LANES, LANES), LANES)
        total = matmul_nt(coupling[0, rows, :], weighted[0])
        total = total + matmul_nt(coupling[1, rows, :], weighted[1])
        system[rows, :] = -total
        return carry

    lax.fori_loop(0, 7, build, 0)
    system[:F, :512] = system[:F, :512] + ordered(4)
    system[F : 2 * F, 384:] = system[F : 2 * F, 384:] + ordered(5)
    coupled = coupled_ref[...].reshape(LANES, F)
    direct = direct_ref[...].reshape(LANES, 2 * F)
    system[2 * F :, :] = direct - matmul_nt(coupled, weighted[place_ref[2]])

    def eliminate(block, carry):
        at = pl.ds(pl.multiple_of(block * LANES, LANES), LANES)
        square = jnp.concatenate(invert([groups_of(system[at, at])])[0], 0)
        panel[...] = matmul(square, system[at, :])
        panel[:, at] = -square

        def update(index, inner):
            rows = pl.ds(pl.multiple_of(index * LANES, LANES), LANES)
            left = system[rows, at]
            system[rows, at] = jnp.zeros((LANES, LANES), jnp.float32)
            system[rows, :] = system[rows, :] - matmul(left, panel[...])
            return inner

        lax.fori_loop(block + 1, 8, update, 0)
        return carry

    lax.fori_loop(0, 7, eliminate, 0)
    solved = system[2 * F :, :]
    same_pair = jnp.where(place_ref[2] == 0, 1.0, 0.0)
    first_ref[...] = same_pair * matmul(coupled, inverse_ref[0]) - matmul(solved, weighted[0])
    second_ref[...] = solved[:, :F]


def output_kernel(first_ref, second_ref, columns_ref, own_ref, out_ref):
    target = lax.broadcasted_iota(jnp.int32, (112, LANES), 0)
    source = lax.broadcasted_iota(jnp.int32, (112, LANES), 1)
    hit = (NODES * (source // 8) + source % 8 == target) & (source % 8 < NODES)
    compact = jnp.where(hit, 1.0, 0.0)
    node = lax.broadcasted_iota(jnp.int32, (F, 512), 0)
    place = lax.broadcasted_iota(jnp.int32, (F, 512), 1)
    hit = (NODES * (place // 8) + place % 8 == node) & (place % 8 < NODES)
    widen = jnp.where(hit, 1.0, 0.0)
    total = matmul(compact, own_ref[...].reshape(LANES, -1))
    for index, ref in enumerate((first_ref, second_ref)):
        rows = matmul(matmul(compact, ref[...]), widen)
        columns = columns_ref[:, index].reshape(512, -1)
        total = total - matmul(rows, columns)
    out_ref[...] = total


def padded(value):
    return jnp.pad(value, [(0, 0)] * (value.ndim - 2) + [(0, 1), (0, 0)])


def other_half(value, axis_part):
    flip = 32 if axis_part == "z" else 1
    return lax.ppermute(value, "tile", [(tile, tile ^ flip) for tile in range(64)])


def to_plane(value):
    value = jnp.stack([value, other_half(value, "z")])
    copies = jnp.broadcast_to(value, (16, *value.shape))
    return lax.all_to_all(
        copies, "tile", split_axis=0, concat_axis=0, tiled=True, axis_index_groups=PLANES
    )


def per_device(box_maps, face_slots):
    stored = box_maps[0]
    box_id = lax.axis_index("box")
    tile_id = lax.axis_index("tile")
    along_x = box_id % 2
    along_y = box_id // 2
    slot_row = lax.dynamic_index_in_dim(face_slots, box_id, 0, keepdims=False)

    def slot_of(surface):
        return lax.dynamic_index_in_dim(slot_row, surface, 0, keepdims=False)

    x_shared = slot_of(1 - along_x)
    y_shared = slot_of(3 - along_y)
    finals = [slot_of(along_x), slot_of(2 + along_y), slot_row[4], slot_row[5]]

    def block(row_slot, col_slot):
        return lax.dynamic_slice(stored, (row_slot, 0, col_slot * F), (1, NODES, F))[0]

    mine = padded(
        jnp.stack([block(x_shared, x_shared), block(y_shared, x_shared), block(y_shared, y_shared)])
    )
    beside_x, other_pair, across = (
        lax.ppermute(mine, "box", [(source, source ^ mask) for source in range(4)])
        for mask in (1, 2, 3)
    )
    squares = jnp.stack([mine[0] + beside_x[0], other_pair[0] + across[0]])
    wide = [(0, 0), (0, 512 - F)]
    shifted = [(0, 0), (512 - F, 0)]
    links = jnp.stack(
        [jnp.pad(part[1], wide) for part in (mine, beside_x, other_pair, across)]
        + [
            jnp.pad(mine[2] + other_pair[2], wide),
            jnp.pad(beside_x[2] + across[2], shifted),
        ]
    )
    squares_own = to_plane(squares)
    squares_other = other_half(squares_own, "core")
    links_own = to_plane(links)
    links_other = other_half(links_own, "core")

    source_box = tile_id // 16
    pair_slot = (source_box // 2) ^ along_y
    side_slot = (source_box % 2) ^ along_x
    places = jnp.stack([tile_id // 32, tile_id % 2, pair_slot]).astype(jnp.int32)

    shared_rows = jnp.stack(
        [
            jnp.concatenate([block(row_slot, col_slot) for col_slot in finals], 1)
            for row_slot in (x_shared, y_shared)
        ]
    )
    columns = lax.all_gather(padded(shared_rows), "tile", axis=0, tiled=False)

    chunks = jnp.stack(
        [
            jnp.stack(
                [
                    jnp.concatenate(
                        [block(row, x_shared), block(row, y_shared), block(row, col)], 1
                    )
                    for col in finals
                ]
            )
            for row in finals
        ]
    ).reshape(16, NODES, 3 * F)
    received = lax.all_to_all(
        padded(chunks),
        "tile",
        split_axis=0,
        concat_axis=0,
        tiled=True,
        axis_index_groups=QUARTERS,
    )
    spread = [
        (64 * box + 16 * quarter + 4 * face + goal, 64 * goal + 16 * box + 4 * face + quarter)
        for box in range(4)
        for quarter in range(4)
        for face in range(4)
        for goal in range(4)
    ]
    row_parts = lax.ppermute(received[:, :, : 2 * F], ("box", "tile"), spread)
    own_parts = []
    for goal in range(4):
        pairs = [
            (64 * box + 16 * quarter + 4 * face + goal, 64 * box + 16 * box + 4 * face + quarter)
            for box in range(4)
            for quarter in range(4)
            for face in range(4)
        ]
        own_parts.append(lax.ppermute(received[:, :, 2 * F :], ("box", "tile"), pairs))
    own_rows = jnp.concatenate(own_parts, 2)
    coupled = row_parts[:, :, :F]
    direct = row_parts[:, :, F:]
    nothing = jnp.zeros_like(direct)
    direct = jnp.where(
        side_slot == 0,
        jnp.concatenate([direct, nothing], 2),
        jnp.concatenate([nothing, direct], 2),
    )

    params = pltpu.CompilerParams(vmem_limit_bytes=VMEM_BYTES)
    smem = pl.BlockSpec(memory_space=pltpu.SMEM)
    vmem = pl.BlockSpec(memory_space=pltpu.VMEM)
    inverse = pl.pallas_call(
        pair_kernel,
        out_shape=jax.ShapeDtypeStruct((2, F, F), jnp.float32),
        in_specs=[smem, vmem, vmem],
        out_specs=vmem,
        scratch_shapes=[
            pltpu.VMEM((2, 512, 512), jnp.float32),
            pltpu.VMEM((2, LANES, 512), jnp.float32),
        ],
        compiler_params=params,
        cost_estimate=pl.CostEstimate(
            flops=20 * 10**9, bytes_accessed=4 * 10**6, transcendentals=0
        ),
        name="invert_pairs",
    )(places, squares_own, squares_other)
    first, second = pl.pallas_call(
        merge_kernel,
        out_shape=[jax.ShapeDtypeStruct((LANES, F), jnp.float32)] * 2,
        in_specs=[smem] + [vmem] * 5,
        out_specs=[vmem] * 2,
        scratch_shapes=[
            pltpu.VMEM((2, 2 * F, F), jnp.float32),
            pltpu.VMEM((2, 2 * F, F), jnp.float32),
            pltpu.VMEM((2 * F + LANES, 2 * F), jnp.float32),
            pltpu.VMEM((LANES, 2 * F), jnp.float32),
        ],
        compiler_params=params,
        cost_estimate=pl.CostEstimate(
            flops=40 * 10**9, bytes_accessed=10 * 10**6, transcendentals=0
        ),
        name="merge_pairs",
    )(places, links_own, links_other, inverse, coupled, direct)
    return pl.pallas_call(
        output_kernel,
        out_shape=jax.ShapeDtypeStruct((112, 4 * F), jnp.float32),
        grid=(7,),
        in_specs=[
            pl.BlockSpec((LANES, F), lambda i: (0, 0)),
            pl.BlockSpec((LANES, F), lambda i: (0, 0)),
            pl.BlockSpec((64, 2, 8, 256), lambda i: (0, 0, 0, i)),
            pl.BlockSpec((16, 8, 256), lambda i: (0, 0, i)),
        ],
        out_specs=pl.BlockSpec((112, 256), lambda i: (0, i)),
        compiler_params=params,
        cost_estimate=pl.CostEstimate(
            flops=4 * 10**9, bytes_accessed=9 * 10**6, transcendentals=0
        ),
        name="final_map",
    )(first, second, columns, own_rows)


def solution(mesh):
    return jax.shard_map(
        per_device,
        mesh=mesh,
        in_specs=(P("box", None, "tile", None), P()),
        out_specs=P("tile", "box"),
        check_vma=False,
    )
```

time: 835 us -> 342 us (0.41)
  the two profiles are of different devices: /device:TPU:33 before, /device:TPU:3 now
where the time goes in v1:
time: 342 us; the launch traced here: 340 us
  Pallas kernels  130 us (38%)
  waiting for transfers between devices  98.1 us (29%)
  starting transfers between devices  45.6 us (13%)
  local copies, waits for them, and re-layouts  33.7 us (10%)
  between operations  28.6 us (8%)
  other arithmetic  4.24 us (1%)
    pallas_call x1, Pallas kernels, per_device(): pl.pallas_call(merge_kernel, out_shape=[jax.ShapeDtypeStruct((LANES, F),...  83.2 us
    ppermute x4, waiting for transfers between devices, per_device(): lax.ppermute(received[:, :, 2 * F:], ('box', 'tile'), pairs)  46.8 us
    pallas_call x1, Pallas kernels, per_device(): pl.pallas_call(pair_kernel, out_shape=jax.ShapeDtypeStruct((2, F, F), jnp...  28.6 us
    all_to_all x2, waiting for transfers between devices, to_plane(): lax.all_to_all(copies, 'tile', split_axis=0, concat_axis=0, tiled=True, a...  28.1 us
    pallas_call x1, Pallas kernels, per_device(): pl.pallas_call(output_kernel, out_shape=jax.ShapeDtypeStruct((112, 4 * F)...  18.5 us
    all_to_all x1, waiting for transfers between devices, per_device(): lax.all_to_all(padded(chunks), 'tile', split_axis=0, concat_axis=0, tiled...  13.3 us
    all_to_all x2, starting transfers between devices, to_plane(): lax.all_to_all(copies, 'tile', split_axis=0, concat_axis=0, tiled=True, a...  11.7 us
    ppermute x4, starting transfers between devices, other_half(): lax.ppermute(value, 'tile', [(tile, tile ^ flip) for tile in range(64)])  9.44 us
  transfers between devices with their start and end apart: 16, of which 10 were waited for; matrix products, arithmetic and copies ran while one was open for 9% of the time, Pallas kernels for 33%

profile of v1, /device:TPU:3, one launch (start us, length us, event | category | flops | bytes accessed | tf_op | source)
XLA Modules:
  0.0 340.5 jit_solution(69709384904224279)
XLA Ops:
  24.2 2.9 constant_dynamic-slice_fusion.4
  29.9 3.0 collective-permute-start.1
  33.0 1.9 collective-permute-done.1
  34.9 3.0 collective-permute-done.2
  38.0 4.5 %collective-permute-start.5 = (f32[2,8,448]{2,0,1:T(2,128)S(1)}, f32[2,8,448]{2,0,1:T(2,128)S(1)}, u32[]{:S(2)}, u32[]{:S(2)}) collective-permute-start(f32[2,8,448]{2,0,1:T(2,128)S(1)} %get-tuple-element.57), channel_id=1, source_target_pairs={{0,32},{1,33},{2,34},{3,35},{4,36},{5,37},{6,38},{7,39},{8,40},{9,... | collective-permute-start | bytes 86024 | tf_op jit(solution)/shard_map/ppermute | solution.py:282
  42.5 2.2 collective-permute-done.5
  46.0 6.9 %all-to-all-start.1 = ((f32[16,2,2,8,448]{4,3,2,1,0:T(8,128)}), f32[16,2,2,8,448]{4,3,2,1,0:T(8,128)S(1)}, u32[]{:S(2)}, u32[]{:S(2)}) async-start(f32[16,2,2,8,448]{4,3,2,1,0:T(8,128)} %broadcast_in_dim.8), calls=%async_computation.1 | async-start | bytes 2097152 | tf_op jit(solution)/shard_map/all_to_all | solution.py:288
  53.0 4.4 %collective-permute-start.3 = (f32[6,8,512]{2,1,0:T(8,128)S(1)}, f32[6,8,512]{2,1,0:T(8,128)S(1)}, u32[]{:S(2)}, u32[]{:S(2)}) collective-permute-start(f32[6,8,512]{2,1,0:T(8,128)S(1)} %bitcast_dynamic-update-slice_fusion), channel_id=1, source_target_pairs={{0,32},{1,33},{2,34},{3,35},{4,36},{5,37},{6,38},{7,39},{8,40},{9,... | collective-permute-start | bytes 294920 | tf_op jit(solution)/shard_map/ppermute | solution.py:282
  57.8 2.6 collective-permute-done.3
  60.4 6.1 %all-to-all-done.1.own_ref = f32[16,2,2,8,448]{4,3,2,1,0:T(8,128)S(1)} async-done(((f32[16,2,2,8,448]{4,3,2,1,0:T(8,128)}), f32[16,2,2,8,448]{4,3,2,1,0:T(8,128)S(1)}, u32[]{:S(2)}, u32[]{:S(2)}) %all-to-all-start.1) | async-done | bytes 917536 | tf_op jit(solution)/shard_map/all_to_all | solution.py:288
  66.6 2.1 broadcast_in_dim.7
  68.7 4.7 %all-to-all-start = ((f32[16,2,6,8,512]{4,3,2,1,0:T(8,128)}), f32[16,2,6,8,512]{4,3,2,1,0:T(8,128)S(1)}, u32[]{:S(2)}, u32[]{:S(2)}) async-start(f32[16,2,6,8,512]{4,3,2,1,0:T(8,128)} %broadcast_in_dim.7), calls=%async_computation | async-start | bytes 6291456 | tf_op jit(solution)/shard_map/all_to_all | solution.py:288
  91.8 22.0 %all-to-all-done.own_ref = f32[16,2,6,8,512]{4,3,2,1,0:T(8,128)S(1)} async-done(((f32[16,2,6,8,512]{4,3,2,1,0:T(8,128)}), f32[16,2,6,8,512]{4,3,2,1,0:T(8,128)S(1)}, u32[]{:S(2)}, u32[]{:S(2)}) %all-to-all-start) | async-done | bytes 3145760 | tf_op jit(solution)/shard_map/all_to_all | solution.py:288
  113.8 9.1 %all-to-all-start.2 = ((f32[16,8,1344]{2,1,0:T(8,128)}), f32[16,8,1344]{2,1,0:T(8,128)}, u32[]{:S(2)}, u32[]{:S(2)}) async-start(f32[16,8,1344]{2,1,0:T(8,128)} %pad.41), calls=%async_computation.2 | async-start | bytes 1441792 | tf_op jit(solution)/shard_map/all_to_all | solution.py:359
  123.4 13.3 %all-to-all-done.2 = f32[16,8,1344]{2,1,0:T(8,128)} async-done(((f32[16,8,1344]{2,1,0:T(8,128)}), f32[16,8,1344]{2,1,0:T(8,128)}, u32[]{:S(2)}, u32[]{:S(2)}) %all-to-all-start.2) | async-done | bytes 688160 | tf_op jit(solution)/shard_map/all_to_all | solution.py:359
  139.7 4.5 %collective-permute-start.11 = (f32[16,8,448]{2,1,0:T(8,128)}, f32[16,8,448]{2,1,0:T(8,128)}, u32[]{:S(2)}, u32[]{:S(2)}) collective-permute-start(f32[16,8,448]{2,1,0:T(8,128)} %slice.92), channel_id=1, source_target_pairs={{3,0},{7,4},{11,8},{15,12},{19,1},{23,5},{27,9},{31,13},{35,2},{39... | collective-permute-start | bytes 688136 | tf_op jit(solution)/shard_map/ppermute | solution.py:383
  144.3 1.8 slice.89
  146.1 2.3 collective-permute-start.7
  148.3 32.0 %collective-permute-done.10 = f32[16,8,448]{2,1,0:T(8,128)S(1)} collective-permute-done((f32[16,8,448]{2,1,0:T(8,128)}, f32[16,8,448]{2,1,0:T(8,128)S(1)}, u32[]{:S(2)}, u32[]{:S(2)}) %collective-permute-start.10) | collective-permute-done | bytes 229408 | tf_op jit(solution)/shard_map/ppermute | solution.py:383
  183.6 14.1 %collective-permute-done.8 = f32[16,8,448]{2,1,0:T(8,128)} collective-permute-done((f32[16,8,448]{2,1,0:T(8,128)}, f32[16,8,448]{2,1,0:T(8,128)}, u32[]{:S(2)}, u32[]{:S(2)}) %collective-permute-start.8) | collective-permute-done | bytes 229408 | tf_op jit(solution)/shard_map/ppermute | solution.py:383
  198.4 2.3 concatenate.83.own_ref
  203.4 28.6 %invert_pairs.1.inverse_ref = f32[2,448,448]{2,1,0:T(8,128)} custom-call(s32[3]{0:T(128)} %pad_add_fusion.place_ref, f32[16,2,2,8,448]{4,3,2,1,0:T(8,128)} %copy-done.1, f32[16,2,2,8,448]{4,3,2,1,0:T(8,128)} %collective-permute-done.6.other_ref), custom_call_target="tpu_custom_call" | custom-call | flops 20000000000 | bytes 4000000 | tf_op jit(solution)/shard_map/invert_pairs/pallas_call | solution.py:397
  231.9 83.2 %merge_pairs.1 = (f32[128,448]{1,0:T(8,128)}, f32[128,448]{1,0:T(8,128)}) custom-call(s32[3]{0:T(128)} %pad_add_fusion.place_ref, f32[16,2,6,8,512]{4,3,2,1,0:T(8,128)} %copy-done, f32[16,2,6,8,512]{4,3,2,1,0:T(8,128)} %collective-permute-done.4.other_ref, f32[2,448,448]{2,1,0:T(8,128)} %invert_pairs.1.inverse_ref, ...), custom_call_target="tpu_custom_call" | custom-call | flops 40000000000 | bytes 10000000 | tf_op jit(solution)/shard_map/merge_pairs/pallas_call | solution.py:412
  315.1 18.5 %final_map.1 = f32[112,1792]{1,0:T(8,128)} custom-call(f32[128,448]{1,0:T(8,128)} %get-tuple-element.7.first_ref, f32[128,448]{1,0:T(8,128)} %get-tuple-element.8.second_ref, f32[64,2,8,1792]{3,2,1,0:T(8,128)} %bitcast.158, f32[16,8,1792]{2,1,0:T(8,128)} %concatenate.83.own_ref), custom_call_target="tpu_custom_call" | custom-call | flops 4000000000 | bytes 9000000 | tf_op jit(solution)/shard_map/final_map/pallas_call | solution.py:429
  (86 shorter events, 35.6 us)
Async XLA Ops:
  6.5 308.6 %all-gather.3.cloned.1.call-start = ((), (), s32[]{:S(2)}) async-start(), calls=%async_computation.3 | async-start | bytes 7454720 | tf_op jit(solution)/shard_map/all_gather | solution.py:344
  28.2 4.7 %collective-permute-start = (f32[3,8,448]{2,1,0:T(8,128)S(1)}, f32[3,8,448]{2,1,0:T(8,128)S(1)}, u32[]{:S(2)}, u32[]{:S(2)}) collective-permute-start(f32[3,8,448]{2,1,0:T(8,128)S(1)} %copy.12), channel_id=1, source_target_pairs={{0,64},{64,0},{128,192},{192,128},{1,65},{65,1},{129,193},{193,129... | collective-permute-start | bytes 129032 | tf_op jit(solution)/shard_map/ppermute | solution.py:315
  29.9 5.0 %collective-permute-start.1 = (f32[3,8,448]{2,1,0:T(8,128)S(1)}, f32[3,8,448]{2,1,0:T(8,128)S(1)}, u32[]{:S(2)}, u32[]{:S(2)}) collective-permute-start(f32[3,8,448]{2,1,0:T(8,128)S(1)} %copy.12), channel_id=1, source_target_pairs={{0,128},{64,192},{128,0},{192,64},{1,129},{65,193},{129,1},{193,65... | collective-permute-start | bytes 129032 | tf_op jit(solution)/shard_map/ppermute | solution.py:315
  32.9 5.0 %collective-permute-start.2 = (f32[3,8,448]{2,0,1:T(4,128)S(1)}, f32[3,8,448]{2,0,1:T(4,128)S(1)}, u32[]{:S(2)}, u32[]{:S(2)}) collective-permute-start(f32[3,8,448]{2,0,1:T(4,128)S(1)} %select_maximum_fusion.1), channel_id=1, source_target_pairs={{0,192},{64,128},{128,64},{192,0},{1,193},{65,129},{129,65},{193,1... | collective-permute-start | bytes 129032 | tf_op jit(solution)/shard_map/ppermute | solution.py:315
  38.0 6.8 %collective-permute-start.5 = (f32[2,8,448]{2,0,1:T(2,128)S(1)}, f32[2,8,448]{2,0,1:T(2,128)S(1)}, u32[]{:S(2)}, u32[]{:S(2)}) collective-permute-start(f32[2,8,448]{2,0,1:T(2,128)S(1)} %get-tuple-element.57), channel_id=1, source_target_pairs={{0,32},{1,33},{2,34},{3,35},{4,36},{5,37},{6,38},{7,39},{8,40},{9,... | collective-permute-start | bytes 86024 | tf_op jit(solution)/shard_map/ppermute | solution.py:282
  46.0 20.6 %all-to-all-start.1 = ((f32[16,2,2,8,448]{4,3,2,1,0:T(8,128)}), f32[16,2,2,8,448]{4,3,2,1,0:T(8,128)S(1)}, u32[]{:S(2)}, u32[]{:S(2)}) async-start(f32[16,2,2,8,448]{4,3,2,1,0:T(8,128)} %broadcast_in_dim.8), calls=%async_computation.1 | async-start | bytes 2097152 | tf_op jit(solution)/shard_map/all_to_all | solution.py:288
  53.0 7.4 %collective-permute-start.3 = (f32[6,8,512]{2,1,0:T(8,128)S(1)}, f32[6,8,512]{2,1,0:T(8,128)S(1)}, u32[]{:S(2)}, u32[]{:S(2)}) collective-permute-start(f32[6,8,512]{2,1,0:T(8,128)S(1)} %bitcast_dynamic-update-slice_fusion), channel_id=1, source_target_pairs={{0,32},{1,33},{2,34},{3,35},{4,36},{5,37},{6,38},{7,39},{8,40},{9,... | collective-permute-start | bytes 294920 | tf_op jit(solution)/shard_map/ppermute | solution.py:282
  66.6 2.1 copy-start.1
  68.7 45.0 %all-to-all-start = ((f32[16,2,6,8,512]{4,3,2,1,0:T(8,128)}), f32[16,2,6,8,512]{4,3,2,1,0:T(8,128)S(1)}, u32[]{:S(2)}, u32[]{:S(2)}) async-start(f32[16,2,6,8,512]{4,3,2,1,0:T(8,128)} %broadcast_in_dim.7), calls=%async_computation | async-start | bytes 6291456 | tf_op jit(solution)/shard_map/all_to_all | solution.py:288
  113.8 89.6 %copy-start = (f32[16,2,6,8,512]{4,3,2,1,0:T(8,128)}, f32[16,2,6,8,512]{4,3,2,1,0:T(8,128)S(1)}, u32[]{:S(2)}) copy-start(f32[16,2,6,8,512]{4,3,2,1,0:T(8,128)S(1)} %all-to-all-done.own_ref) | copy-start | bytes 9437188
  113.8 23.0 %all-to-all-start.2 = ((f32[16,8,1344]{2,1,0:T(8,128)}), f32[16,8,1344]{2,1,0:T(8,128)}, u32[]{:S(2)}, u32[]{:S(2)}) async-start(f32[16,8,1344]{2,1,0:T(8,128)} %pad.41), calls=%async_computation.2 | async-start | bytes 1441792 | tf_op jit(solution)/shard_map/all_to_all | solution.py:359
  122.9 109.0 %collective-permute-start.4 = (f32[16,2,6,8,512]{4,3,2,1,0:T(8,128)S(1)}, f32[16,2,6,8,512]{4,3,2,1,0:T(8,128)}, u32[]{:S(2)}, u32[]{:S(2)}) collective-permute-start(f32[16,2,6,8,512]{4,3,2,1,0:T(8,128)S(1)} %all-to-all-done.own_ref), channel_id=1, source_target_pairs={{0,1},{1,0},{2,3},{3,2},{4,5},{5,4},{6,7},{7,6},{8,9},{9,8},{10,11... | collective-permute-start | bytes 9437192 | tf_op jit(solution)/shard_map/ppermute | solution.py:282
  123.3 80.1 %collective-permute-start.6 = (f32[16,2,2,8,448]{4,3,2,1,0:T(8,128)}, f32[16,2,2,8,448]{4,3,2,1,0:T(8,128)}, u32[]{:S(2)}, u32[]{:S(2)}) collective-permute-start(f32[16,2,2,8,448]{4,3,2,1,0:T(8,128)} %copy-done.1), channel_id=1, source_target_pairs={{0,1},{1,0},{2,3},{3,2},{4,5},{5,4},{6,7},{7,6},{8,9},{9,8},{10,11... | collective-permute-start | bytes 2752520 | tf_op jit(solution)/shard_map/ppermute | solution.py:282
  138.4 41.9 %collective-permute-start.10 = (f32[16,8,448]{2,1,0:T(8,128)}, f32[16,8,448]{2,1,0:T(8,128)S(1)}, u32[]{:S(2)}, u32[]{:S(2)}) collective-permute-start(f32[16,8,448]{2,1,0:T(8,128)} %slice.92), channel_id=1, source_target_pairs={{2,0},{6,4},{10,8},{14,12},{18,1},{22,5},{26,9},{30,13},{34,2},{38... | collective-permute-start | bytes 688136 | tf_op jit(solution)/shard_map/ppermute | solution.py:383
  139.7 41.9 %collective-permute-start.11 = (f32[16,8,448]{2,1,0:T(8,128)}, f32[16,8,448]{2,1,0:T(8,128)}, u32[]{:S(2)}, u32[]{:S(2)}) collective-permute-start(f32[16,8,448]{2,1,0:T(8,128)} %slice.92), channel_id=1, source_target_pairs={{3,0},{7,4},{11,8},{15,12},{19,1},{23,5},{27,9},{31,13},{35,2},{39... | collective-permute-start | bytes 688136 | tf_op jit(solution)/shard_map/ppermute | solution.py:383
  146.1 54.6 %collective-permute-start.7 = (f32[16,8,896]{2,1,0:T(8,128)}, f32[16,8,896]{2,1,0:T(8,128)}, u32[]{:S(2)}, u32[]{:S(2)}) collective-permute-start(f32[16,8,896]{2,1,0:T(8,128)} %slice.89), channel_id=1, source_target_pairs={{0,0},{1,64},{2,128},{3,192},{4,4},{5,68},{6,132},{7,196},{8,8},{9... | collective-permute-start | bytes 1376264 | tf_op jit(solution)/shard_map/ppermute | solution.py:374
  180.4 17.3 %collective-permute-start.8 = (f32[16,8,448]{2,1,0:T(8,128)}, f32[16,8,448]{2,1,0:T(8,128)}, u32[]{:S(2)}, u32[]{:S(2)}) collective-permute-start(f32[16,8,448]{2,1,0:T(8,128)} %slice.92), channel_id=1, source_target_pairs={{0,0},{4,4},{8,8},{12,12},{16,1},{20,5},{24,9},{28,13},{32,2},{36,... | collective-permute-start | bytes 688136 | tf_op jit(solution)/shard_map/ppermute | solution.py:383
  181.7 16.7 %collective-permute-start.9 = (f32[16,8,448]{2,1,0:T(8,128)}, f32[16,8,448]{2,1,0:T(8,128)}, u32[]{:S(2)}, u32[]{:S(2)}) collective-permute-start(f32[16,8,448]{2,1,0:T(8,128)} %slice.92), channel_id=1, source_target_pairs={{1,0},{5,4},{9,8},{13,12},{17,1},{21,5},{25,9},{29,13},{33,2},{37,... | collective-permute-start | bytes 688136 | tf_op jit(solution)/shard_map/ppermute | solution.py:383
Sparse Core Ops, SparseCore 0:
  28.2 154.7 all-gather.2

commit v2 on v1

v2 whole, which is shorter than its diff:
```python
import functools

import jax
import jax.numpy as jnp
from jax import lax
from jax.experimental import pallas as pl
from jax.experimental.pallas import tpu as pltpu
from jax.sharding import PartitionSpec as P

F = 448
NODES = 7
LANES = 128
MICRO = 16
VMEM_BYTES = 56 * 1024 * 1024


def tile_of(z, y, x, core):
    return ((z * 4 + y) * 4 + x) * 2 + core


PLANES = [
    [tile_of(z, y, x, core) for y in range(4) for x in range(4)]
    for z in range(2)
    for core in range(2)
]
QUARTERS = [[16 * quarter + own for own in range(16)] for quarter in range(4)]


def matmul(left, right):
    return jnp.dot(left, right, precision=lax.Precision.HIGHEST, preferred_element_type=jnp.float32)


def halves(value):
    high = value.astype(jnp.bfloat16)
    return high, (value - high.astype(jnp.float32)).astype(jnp.bfloat16)


def left_parts(value):
    high, low = halves(value)
    return jnp.concatenate([high, high, low], 1)


def right_parts(value, dim=0):
    high, low = halves(value)
    return jnp.concatenate([high, low, high], dim)


def split_matmul(left, right):
    return jnp.dot(left, right, preferred_element_type=jnp.float32)


def split_matmul_nt(left, right):
    return lax.dot_general(
        left, right, (((1,), (1,)), ((), ())), preferred_element_type=jnp.float32
    )


def invert(stack):
    full = (8, LANES)
    lane = lax.broadcasted_iota(jnp.int32, full, 1)
    sub = lax.broadcasted_iota(jnp.int32, full, 0)

    def along_rows(value, row):
        return jnp.broadcast_to(value[row : row + 1, :], full)

    def along_lanes(value, column):
        return jnp.broadcast_to(value[:, column : column + 1], full)

    stack = [list(rows) for rows in stack]
    count = len(stack[0])
    which = range(len(stack))
    for start in range(0, 8 * count, MICRO):
        first = start // 8
        inside = (lane >= start) & (lane < start + MICRO)
        following = [group for group in (first + 2, first + 3) if group < count]
        rest = [g for g in range(count) if g not in (first, first + 1, *following)]
        pivots = [
            [[along_lanes(stack[n][first + h], start + k) for h in range(2)] for k in range(MICRO)]
            for n in which
        ]
        rows = [
            [
                jnp.where(
                    inside,
                    jnp.where(lane == start + 8 * h + sub, 1.0, 0.0),
                    stack[n][first + h],
                )
                for h in range(2)
            ]
            for n in which
        ]
        ahead = [
            [[along_lanes(stack[n][group], start + k) for k in range(MICRO)] for group in following]
            for n in which
        ]
        for j in range(MICRO):
            half, row = divmod(j, 8)
            chosen = sub == row
            for n in which:
                scale = 1.0 / along_rows(pivots[n][j][half], row)
                pivot_row = along_rows(rows[n][half], row) * scale
                for k in range(j + 1, MICRO):
                    scaled = along_rows(pivots[n][k][half], row) * scale
                    for h in range(2):
                        value = pivots[n][k][h] - pivots[n][j][h] * scaled
                        pivots[n][k][h] = jnp.where(chosen, scaled, value) if h == half else value
                for h in range(2):
                    value = rows[n][h] - pivots[n][j][h] * pivot_row
                    rows[n][h] = jnp.where(chosen, pivot_row, value) if h == half else value
        for n in which:
            spread = [along_rows(rows[n][k // 8], k % 8) for k in range(MICRO)]
            for position, group in enumerate(following):
                terms = [ahead[n][position][k] * spread[k] for k in range(MICRO)]
                while len(terms) > 1:
                    terms = [terms[i] + terms[i + 1] for i in range(0, len(terms), 2)]
                stack[n][group] = jnp.where(inside, 0.0, stack[n][group]) - terms[0]
            if rest:
                zero = jnp.zeros(full, jnp.float32)
                held = jnp.concatenate([stack[n][group] for group in rest], 0)
                panel = jnp.concatenate(
                    [zero] * first + rows[n] + [zero] * (LANES // 8 - first - 2), 0
                )
                update = matmul(held, panel)
                for i, group in enumerate(rest):
                    stack[n][group] = (
                        jnp.where(inside, 0.0, stack[n][group]) - update[8 * i : 8 * i + 8]
                    )
            stack[n][first], stack[n][first + 1] = rows[n]
    return stack


def groups_of(value):
    return [value[8 * g : 8 * g + 8, :] for g in range(value.shape[0] // 8)]


def node_orders():
    tile = lax.axis_index("tile")
    core = tile % 2
    shape = (F, 256)
    target = lax.broadcasted_iota(jnp.int32, shape, 0)
    source = lax.broadcasted_iota(jnp.int32, shape, 1)
    inner = source % 8
    half = (source // 8) % 2
    half = jnp.where(tile >= 32, 1 - half, half)
    orders = []
    for held_core in (core, 1 - core):
        node = NODES * ((half * 16 + source // 16) * 2 + held_core) + inner
        hit = (node == target) & (inner < NODES)
        orders.append(jnp.where(hit, 1.0, 0.0).astype(jnp.bfloat16))
    return orders


def in_node_order(orders, pieces):
    total = None
    for order, piece in zip(orders, pieces):
        for _ in range(3):
            part = piece.astype(jnp.bfloat16)
            piece = piece - part.astype(jnp.float32)
            term = jnp.dot(order, part, preferred_element_type=jnp.float32)
            total = term if total is None else total + term
    return total


def pair_kernel(own_ref, other_ref, inverse_ref, work, panel):
    orders = node_orders()
    for n in range(2):
        pieces = [ref[:, :, n].reshape(256, 512) for ref in (own_ref, other_ref)]
        work[n, :F, :] = in_node_order(orders, pieces)
        work[n, F:, :] = jnp.zeros((512 - F, 512), jnp.float32)

    def eliminate(block, height):
        at = pl.ds(pl.multiple_of(block * LANES, LANES), LANES)
        squares = [groups_of(work[n, at, at])[: height // 8] for n in range(2)]
        inverses = invert(squares)
        for n in range(2):
            square = jnp.concatenate(inverses[n], 0)
            if height < LANES:
                square = jnp.concatenate(
                    [square, jnp.zeros((LANES - height, LANES), jnp.float32)], 0
                )
            left = left_parts(work[n, :, at])
            scaled = split_matmul(left_parts(square), right_parts(work[n, at, :]))
            work[n, :, at] = jnp.zeros((512, LANES), jnp.float32)
            panel[n] = scaled
            panel[n, :, at] = square
            scaled = panel[n]
            work[n] = work[n] - split_matmul(left, right_parts(scaled))
            work[n, at, :] = scaled

    def step(block, carry):
        eliminate(block, LANES)
        return carry

    lax.fori_loop(0, 3, step, 0)
    eliminate(jnp.int32(3), F - 3 * LANES)
    inverse_ref[...] = work[:, :F, :]


def merge_kernel(
    own_ref,
    other_ref,
    inverse_ref,
    rows_ref,
    first_ref,
    second_ref,
    coupling,
    weighted,
    system,
    panel,
):
    tile = lax.axis_index("tile")
    box = lax.axis_index("box")
    source_box = tile // 16
    pair_slot = jnp.where(source_box // 2 == box // 2, 0, 1)
    side_slot = jnp.where(source_box % 2 == box % 2, 0, 1)
    orders = node_orders()

    def ordered(index):
        pieces = [ref[:, :, index].reshape(256, 512) for ref in (own_ref, other_ref)]
        return in_node_order(orders, pieces)

    for pair in range(2):
        square = right_parts(
            jnp.concatenate([inverse_ref[pair], jnp.zeros((512 - F, 512), jnp.float32)], 0)
        )
        for side in range(2):
            at = pl.ds(side * F, F)
            left = left_parts(ordered(2 * pair + side))
            coupling[pair, at, :] = left
            weighted[pair, at, :] = right_parts(split_matmul(left, square), 1)

    for half in range(2):
        at = pl.ds(half * F, F)
        total = split_matmul_nt(coupling[0, at, :], weighted[0])
        system[at, :] = -total - split_matmul_nt(coupling[1, at, :], weighted[1])
    system[:F, :512] = system[:F, :512] + ordered(4)
    system[F : 2 * F, 384:] = system[F : 2 * F, 384:] + ordered(5)
    coupled = jnp.concatenate(
        [rows_ref[:, :, :F].reshape(LANES, F), jnp.zeros((LANES, 512 - F), jnp.float32)], 1
    )
    coupled_parts = left_parts(coupled)
    system[2 * F :, :] = -split_matmul_nt(coupled_parts, weighted[pair_slot])
    direct = rows_ref[:, :, F : 2 * F].reshape(LANES, F)
    gap = jnp.zeros((LANES, 512 - F), jnp.float32)

    @pl.when(side_slot == 0)
    def _():
        system[2 * F :, :512] = system[2 * F :, :512] + jnp.concatenate([direct, gap], 1)

    @pl.when(side_slot == 1)
    def _():
        system[2 * F :, 384:] = system[2 * F :, 384:] + jnp.concatenate([gap, direct], 1)

    def eliminate(block, carry):
        at = pl.ds(pl.multiple_of(block * LANES, LANES), LANES)
        square = jnp.concatenate(invert([groups_of(system[at, at])])[0], 0)
        scaled = split_matmul(left_parts(square), right_parts(system[at, :]))
        high, low = halves(scaled)
        panel[:LANES] = high
        panel[LANES : 2 * LANES] = low
        high, low = halves(-square)
        panel[:LANES, at] = high
        panel[LANES : 2 * LANES, at] = low
        panel[2 * LANES :] = panel[:LANES]

        def update(start, count):
            rows = pl.ds(pl.multiple_of(start * LANES, LANES), count * LANES)
            left = left_parts(system[rows, at])
            system[rows, at] = jnp.zeros((count * LANES, LANES), jnp.float32)
            system[rows, :] = system[rows, :] - split_matmul(left, panel[...])

        def pairwise(index, inner):
            update(6 - 2 * index, 2)
            return inner

        lax.fori_loop(0, (7 - block) // 2, pairwise, 0)

        @pl.when((7 - block) % 2 == 1)
        def _():
            update(block + 1, 1)

        return carry

    lax.fori_loop(0, 7, eliminate, 0)
    solved = system[2 * F :, :]
    same_pair = jnp.where(pair_slot == 0, 1.0, 0.0)
    square = right_parts(
        jnp.concatenate([inverse_ref[0], jnp.zeros((512 - F, 512), jnp.float32)], 0)
    )
    high = weighted[0, :, :512]
    low = weighted[0, :, 512:1024]
    first = same_pair * split_matmul(coupled_parts, square)
    first = first - split_matmul(left_parts(solved), jnp.concatenate([high, low, high], 0))
    first_ref[...] = first[:, :F]
    second_ref[...] = solved[:, :F]


def output_kernel(first_ref, second_ref, own_ref, other_ref, rows_ref, out_ref, spread):
    @pl.when(pl.program_id(0) == 0)
    def _():
        target = lax.broadcasted_iota(jnp.int32, (112, LANES), 0)
        source = lax.broadcasted_iota(jnp.int32, (112, LANES), 1)
        hit = (NODES * (source // 8) + source % 8 == target) & (source % 8 < NODES)
        compact = jnp.where(hit, 1.0, 0.0)
        orders = node_orders()
        for index, ref in enumerate((first_ref, second_ref)):
            high, low = halves(matmul(compact, ref[...]))
            for place, order in enumerate(orders):
                for part, value in enumerate((high, high, low)):
                    moved = jnp.dot(value, order, preferred_element_type=jnp.float32)
                    spread[index, place, part] = moved.astype(jnp.bfloat16)

    target = lax.broadcasted_iota(jnp.int32, (112, LANES), 0)
    source = lax.broadcasted_iota(jnp.int32, (112, LANES), 1)
    hit = (NODES * (source // 8) + source % 8 == target) & (source % 8 < NODES)
    compact = jnp.where(hit, 1.0, 0.0)
    total = matmul(compact, rows_ref[...].reshape(LANES, -1))
    lefts = []
    rights = []
    for index in range(2):
        for place, ref in enumerate((own_ref, other_ref)):
            lefts += [spread[index, place, part] for part in range(3)]
            rights.append(right_parts(ref[:, :, index].reshape(256, -1)))
    total = total - split_matmul(jnp.concatenate(lefts, 1), jnp.concatenate(rights, 0))
    out_ref[...] = total


def select_kernel(slots_ref, stored_ref, mine_ref, shared_ref, rows_ref):
    box = lax.axis_index("box")
    along_x = box % 2
    along_y = box // 2
    x_shared = slots_ref[box, 1 - along_x]
    y_shared = slots_ref[box, 3 - along_y]
    finals = [
        slots_ref[box, along_x],
        slots_ref[box, 2 + along_y],
        slots_ref[box, 4],
        slots_ref[box, 5],
    ]
    lane = lax.broadcasted_iota(jnp.int32, (8, 512), 1)

    def block(row_slot, col_slot):
        start = pl.multiple_of(((col_slot * 7) // 2) * LANES, LANES)
        value = stored_ref[row_slot, :, pl.ds(start, 512)]
        value = jnp.concatenate([value, jnp.zeros((1, 512), jnp.float32)], 0)
        value = jnp.where(col_slot % 2 == 1, pltpu.roll(value, F, 1), value)
        return jnp.where(lane < F, value, 0.0)

    mine_ref[0] = block(x_shared, x_shared)
    mine_ref[1] = block(y_shared, x_shared)
    mine_ref[2] = block(y_shared, y_shared)
    for index, row_slot in enumerate((x_shared, y_shared)):
        for place, col_slot in enumerate(finals):
            shared_ref[index, :, place * F : place * F + F] = block(row_slot, col_slot)[:, :F]
    for index, row_slot in enumerate(finals):
        for place, col_slot in enumerate((x_shared, y_shared, *finals)):
            rows_ref[index, :, place * F : place * F + F] = block(row_slot, col_slot)[:, :F]


def combine_kernel(mine_ref, beside_ref, other_ref, across_ref, out_ref):
    out_ref[0] = mine_ref[0] + beside_ref[0]
    out_ref[1] = other_ref[0] + across_ref[0]
    for index, ref in enumerate((mine_ref, beside_ref, other_ref, across_ref)):
        out_ref[2 + index] = ref[1]
    out_ref[6] = mine_ref[2] + other_ref[2]
    out_ref[7] = pltpu.roll(beside_ref[2] + across_ref[2], 512 - F, 1)


def other_half(value, axis_part):
    flip = 32 if axis_part == "z" else 1
    return lax.ppermute(value, "tile", [(tile, tile ^ flip) for tile in range(64)])


def to_plane(value):
    copies = jnp.broadcast_to(value, (16, *value.shape))
    return lax.all_to_all(
        copies, "tile", split_axis=0, concat_axis=0, tiled=True, axis_index_groups=PLANES
    )


def kernel_call(body, out_shapes, name, micros, **options):
    return pl.pallas_call(
        body,
        out_shape=[jax.ShapeDtypeStruct(shape, jnp.float32) for shape in out_shapes],
        compiler_params=pltpu.CompilerParams(vmem_limit_bytes=VMEM_BYTES),
        cost_estimate=pl.CostEstimate(
            flops=micros * 10**9, bytes_accessed=10**6, transcendentals=0
        ),
        name=name,
        **options,
    )


def per_device(box_maps, face_slots):
    smem = pl.BlockSpec(memory_space=pltpu.SMEM)
    vmem = pl.BlockSpec(memory_space=pltpu.VMEM)
    mine, shared_rows, outer_rows = kernel_call(
        select_kernel,
        [(3, 8, 512), (2, 8, 4 * F), (4, 8, 6 * F)],
        "select_rows",
        2,
        in_specs=[smem, vmem],
        out_specs=[vmem] * 3,
    )(face_slots, box_maps[0])
    parts = [
        lax.ppermute(mine, "box", [(source, source ^ mask) for source in range(4)])
        for mask in (1, 2, 3)
    ]
    (raw,) = kernel_call(
        combine_kernel, [(8, 8, 512)], "combine_boxes", 1, in_specs=[vmem] * 4, out_specs=[vmem]
    )(mine, *parts)
    raw = jnp.stack([raw, other_half(raw, "z")])
    squares_own = to_plane(raw[:, :2])
    squares_other = other_half(squares_own, "core")
    links_own = to_plane(raw[:, 2:])

    goals = jnp.broadcast_to(outer_rows[:, None], (4, 4, 8, 6 * F)).reshape(16, 8, 6 * F)
    received = lax.all_to_all(
        goals, "tile", split_axis=0, concat_axis=0, tiled=True, axis_index_groups=QUARTERS
    )
    spread = [
        (64 * box + 16 * quarter + 4 * face + goal, 64 * goal + 16 * box + 4 * face + quarter)
        for box in range(4)
        for quarter in range(4)
        for face in range(4)
        for goal in range(4)
    ]
    row_parts = lax.ppermute(received[:, :, : 2 * F], ("box", "tile"), spread)
    own_rows = lax.ppermute(
        received[:, :, 2 * F :],
        ("box", "tile"),
        [pair for pair in spread if pair[0] // 64 == pair[1] // 64],
    )
    columns_own = to_plane(jnp.stack([shared_rows, other_half(shared_rows, "z")]))

    (inverse,) = kernel_call(
        pair_kernel,
        [(2, F, 512)],
        "invert_pairs",
        20,
        in_specs=[vmem] * 2,
        out_specs=[vmem],
        scratch_shapes=[
            pltpu.VMEM((2, 512, 512), jnp.float32),
            pltpu.VMEM((2, LANES, 512), jnp.float32),
        ],
    )(squares_own, squares_other)
    inverse, links_own = lax.optimization_barrier((inverse, links_own))
    links_other = other_half(links_own, "core")
    columns_other = other_half(columns_own, "core")
    first, second = kernel_call(
        merge_kernel,
        [(LANES, F)] * 2,
        "merge_pairs",
        45,
        in_specs=[vmem] * 4,
        out_specs=[vmem] * 2,
        scratch_shapes=[
            pltpu.VMEM((2, 2 * F, 3 * 512), jnp.bfloat16),
            pltpu.VMEM((2, 2 * F, 3 * 512), jnp.bfloat16),
            pltpu.VMEM((2 * F + LANES, 2 * F), jnp.float32),
            pltpu.VMEM((3 * LANES, 2 * F), jnp.bfloat16),
        ],
    )(links_own, links_other, inverse, row_parts)
    (out,) = kernel_call(
        output_kernel,
        [(112, 4 * F)],
        "final_map",
        6,
        grid=(7,),
        in_specs=[
            pl.BlockSpec((LANES, F), lambda i: (0, 0)),
            pl.BlockSpec((LANES, F), lambda i: (0, 0)),
            pl.BlockSpec((16, 2, 2, 8, 256), lambda i: (0, 0, 0, 0, i)),
            pl.BlockSpec((16, 2, 2, 8, 256), lambda i: (0, 0, 0, 0, i)),
            pl.BlockSpec((16, 8, 256), lambda i: (0, 0, i)),
        ],
        out_specs=[pl.BlockSpec((112, 256), lambda i: (0, i))],
        scratch_shapes=[pltpu.VMEM((2, 2, 3, 112, 256), jnp.bfloat16)],
    )(first, second, columns_own, columns_other, own_rows)
    return out


def solution(mesh):
    return jax.shard_map(
        per_device,
        mesh=mesh,
        in_specs=(P("box", None, "tile", None), P()),
        out_specs=P("tile", "box"),
        check_vma=False,
    )
```

time: 342 us -> 267 us (0.78)
  the two profiles are of different devices: /device:TPU:3 before, /device:TPU:33 now
where the time goes in v2:
time: 267 us; the launch traced here: 263 us
  waiting for transfers between devices  100 us (37%)
  Pallas kernels  84.1 us (31%)
  starting transfers between devices  47.8 us (18%)
  blocking collectives  18.6 us (7%)
  local copies, waits for them, and re-layouts  11.1 us (4%)
    all_to_all x2, waiting for transfers between devices, to_plane(): lax.all_to_all(copies, 'tile', split_axis=0, concat_axis=0, tiled=True, a...  70.9 us
    pallas_call x1, Pallas kernels, per_device(): kernel_call(merge_kernel, [(LANES, F)] * 2, 'merge_pairs', 45, in_specs=[...  47.3 us
    pallas_call x1, Pallas kernels, per_device(): kernel_call(pair_kernel, [(2, F, 512)], 'invert_pairs', 20, in_specs=[vme...  23.7 us
    all_to_all x1, waiting for transfers between devices, per_device(): lax.all_to_all(goals, 'tile', split_axis=0, concat_axis=0, tiled=True, ax...  19.4 us
    all_to_all x1, blocking collectives, to_plane(): lax.all_to_all(copies, 'tile', split_axis=0, concat_axis=0, tiled=True, a...  18.6 us
    ppermute x5, starting transfers between devices, other_half(): lax.ppermute(value, 'tile', [(tile, tile ^ flip) for tile in range(64)])  14.9 us
    all_to_all x1, starting transfers between devices, per_device(): lax.all_to_all(goals, 'tile', split_axis=0, concat_axis=0, tiled=True, ax...  10.2 us
    all_to_all x2, starting transfers between devices, to_plane(): lax.all_to_all(copies, 'tile', split_axis=0, concat_axis=0, tiled=True, a...  9.3 us
  transfers between devices with their start and end apart: 13, of which 7 were waited for; matrix products, arithmetic and copies ran while one was open for 1% of the time, Pallas kernels for 27%

profile of v2, /device:TPU:33, one launch (start us, length us, event | category | flops | bytes accessed | tf_op | source)
XLA Modules:
  0.0 262.6 jit_solution(16930870295742544471)
XLA Ops:
  0.0 1.9 copy.5
  1.9 2.4 select_rows.1
  4.3 1.6 collective-permute-start.2
  10.0 1.7 collective-permute-done.beside_ref
  12.3 1.6 combine_boxes.1
  13.9 5.2 %collective-permute-start.3 = (f32[8,8,512]{2,1,0:T(8,128)}, f32[8,8,512]{2,1,0:T(8,128)S(1)}, u32[]{:S(2)}, u32[]{:S(2)}) collective-permute-start(f32[8,8,512]{2,1,0:T(8,128)} %combine_boxes.1), channel_id=1, source_target_pairs={{0,32},{1,33},{2,34},{3,35},{4,36},{5,37},{6,38},{7,39},{8,40},{9,... | collective-permute-start | bytes 393224 | tf_op jit(solution)/shard_map/ppermute | solution.py:371
  19.2 2.7 %collective-permute-done.3 = f32[8,8,512]{2,1,0:T(8,128)S(1)} collective-permute-done((f32[8,8,512]{2,1,0:T(8,128)}, f32[8,8,512]{2,1,0:T(8,128)S(1)}, u32[]{:S(2)}, u32[]{:S(2)}) %collective-permute-start.3) | collective-permute-done | bytes 131104 | tf_op jit(solution)/shard_map/ppermute | solution.py:371
  22.8 18.6 %all_to_all.20.own_ref = f32[16,2,2,8,512]{4,3,2,1,0:T(8,128)S(1)} all-to-all(f32[16,2,2,8,512]{4,3,2,1,0:T(8,128)S(1)} %broadcast_in_dim.15), channel_id=1, replica_groups={{0,2,4,6,8,10,12,14,16,18,20,22,24,26,28,30},{1,3,5,7,9,11,13,15,17,19,..., dimensions={0} | all-to-all | bytes 2097152 | tf_op jit(solution)/shard_map/all_to_all | solution.py:376
  42.7 10.2 %all-to-all-start.2 = ((f32[16,8,2688]{2,1,0:T(8,128)}), f32[16,8,2688]{2,1,0:T(8,128)S(1)}, u32[]{:S(2)}, u32[]{:S(2)}) async-start(f32[16,8,2688]{2,1,0:T(8,128)} %bitcast.2), calls=%async_computation.2 | async-start | bytes 2752512 | tf_op jit(solution)/shard_map/all_to_all | solution.py:418
  52.9 19.4 %all-to-all-done.2 = f32[16,8,2688]{2,1,0:T(8,128)S(1)} async-done(((f32[16,8,2688]{2,1,0:T(8,128)}), f32[16,8,2688]{2,1,0:T(8,128)S(1)}, u32[]{:S(2)}, u32[]{:S(2)}) %all-to-all-start.2) | async-done | bytes 1376288 | tf_op jit(solution)/shard_map/all_to_all | solution.py:418
  72.4 2.0 broadcast_in_dim.16
  74.4 4.6 %all-to-all-start.1 = ((f32[16,2,6,8,512]{4,3,2,1,0:T(8,128)}), f32[16,2,6,8,512]{4,3,2,1,0:T(8,128)}, u32[]{:S(2)}, u32[]{:S(2)}) async-start(f32[16,2,6,8,512]{4,3,2,1,0:T(8,128)} %broadcast_in_dim.16), calls=%async_computation.1 | async-start | bytes 6291456 | tf_op jit(solution)/shard_map/all_to_all | solution.py:376
  79.8 4.9 %collective-permute-start.7 = (f32[2,8,1792]{2,1,0:T(8,128)S(1)}, f32[2,8,1792]{2,1,0:T(8,128)S(1)}, u32[]{:S(2)}, u32[]{:S(2)}) collective-permute-start(f32[2,8,1792]{2,1,0:T(8,128)S(1)} %copy-done.3), channel_id=1, source_target_pairs={{0,32},{1,33},{2,34},{3,35},{4,36},{5,37},{6,38},{7,39},{8,40},{9,... | collective-permute-start | bytes 344072 | tf_op jit(solution)/shard_map/ppermute | solution.py:371
  84.8 3.8 %collective-permute-done.7 = f32[2,8,1792]{2,1,0:T(8,128)S(1)} collective-permute-done((f32[2,8,1792]{2,1,0:T(8,128)S(1)}, f32[2,8,1792]{2,1,0:T(8,128)S(1)}, u32[]{:S(2)}, u32[]{:S(2)}) %collective-permute-start.7) | collective-permute-done | bytes 114720 | tf_op jit(solution)/shard_map/ppermute | solution.py:371
  88.6 37.8 %all-to-all-done.1.own_ref = f32[16,2,6,8,512]{4,3,2,1,0:T(8,128)} async-done(((f32[16,2,6,8,512]{4,3,2,1,0:T(8,128)}), f32[16,2,6,8,512]{4,3,2,1,0:T(8,128)}, u32[]{:S(2)}, u32[]{:S(2)}) %all-to-all-start.1) | async-done | bytes 3145760 | tf_op jit(solution)/shard_map/all_to_all | solution.py:376
  126.4 2.2 broadcast_in_dim.18
  128.6 4.7 %all-to-all-start.3 = ((f32[16,2,2,8,1792]{4,3,2,1,0:T(8,128)}), f32[16,2,2,8,1792]{4,3,2,1,0:T(8,128)}, u32[]{:S(2)}, u32[]{:S(2)}) async-start(f32[16,2,2,8,1792]{4,3,2,1,0:T(8,128)} %broadcast_in_dim.18), calls=%async_computation.3 | async-start | bytes 7340032 | tf_op jit(solution)/shard_map/all_to_all | solution.py:376
  133.4 23.7 %invert_pairs.1.inverse_ref = f32[2,448,512]{2,1,0:T(8,128)} custom-call(f32[16,2,2,8,512]{4,3,2,1,0:T(8,128)} %copy-done, f32[16,2,2,8,512]{4,3,2,1,0:T(8,128)} %collective-permute-done.4.other_ref), custom_call_target="tpu_custom_call" | custom-call | flops 20000000000 | bytes 1000000 | tf_op jit(solution)/shard_map/invert_pairs/pallas_call | solution.py:436
  158.7 4.7 %collective-permute-start.6 = (f32[16,8,896]{2,1,0:T(8,128)S(1)}, f32[16,8,896]{2,1,0:T(8,128)S(1)}, u32[]{:S(2)}, u32[]{:S(2)}) collective-permute-start(f32[16,8,896]{2,1,0:T(8,128)S(1)} %slice.16), channel_id=1, source_target_pairs={{0,0},{1,64},{2,128},{3,192},{4,4},{5,68},{6,132},{7,196},{8,8},{9... | collective-permute-start | bytes 1376264 | tf_op jit(solution)/shard_map/ppermute | solution.py:428
  163.4 4.5 %collective-permute-start.9 = (f32[16,8,1792]{2,1,0:T(8,128)S(1)}, f32[16,8,1792]{2,1,0:T(8,128)S(1)}, u32[]{:S(2)}, u32[]{:S(2)}) collective-permute-start(f32[16,8,1792]{2,1,0:T(8,128)S(1)} %slice.17), channel_id=1, source_target_pairs={{0,0},{4,4},{8,8},{12,12},{16,1},{20,5},{24,9},{28,13},{32,2},{36,... | collective-permute-start | bytes 2752520 | tf_op jit(solution)/shard_map/ppermute | solution.py:429
  167.9 33.1 %all-to-all-done.3.own_ref = f32[16,2,2,8,1792]{4,3,2,1,0:T(8,128)} async-done(((f32[16,2,2,8,1792]{4,3,2,1,0:T(8,128)}), f32[16,2,2,8,1792]{4,3,2,1,0:T(8,128)}, u32[]{:S(2)}, u32[]{:S(2)}) %all-to-all-start.3) | async-done | bytes 3670048 | tf_op jit(solution)/shard_map/all_to_all | solution.py:376
  201.0 2.4 collective-permute-start.8
  204.2 47.3 %merge_pairs.1 = (f32[128,448]{1,0:T(8,128)}, f32[128,448]{1,0:T(8,128)}) custom-call(f32[16,2,6,8,512]{4,3,2,1,0:T(8,128)} %all-to-all-done.1.own_ref, f32[16,2,6,8,512]{4,3,2,1,0:T(8,128)} %collective-permute-done.5.other_ref, f32[2,448,512]{2,1,0:T(8,128)} %invert_pairs.1.inverse_ref, f32[16,8,896]{2,1,0:T(8,128)} %copy-done.6), custom_call_target="tpu_custom_call" | custom-call | flops 44999999488 | bytes 1000000 | tf_op jit(solution)/shard_map/merge_pairs/pallas_call | solution.py:451
  253.6 9.0 %final_map.1 = f32[112,1792]{1,0:T(8,128)} custom-call(f32[128,448]{1,0:T(8,128)} %get-tuple-element.16.first_ref, f32[128,448]{1,0:T(8,128)} %get-tuple-element.17.second_ref, f32[16,2,2,8,1792]{4,3,2,1,0:T(8,128)} %all-to-all-done.3.own_ref, f32[16,2,2,8,1792]{4,3,2,1,0:T(8,128)} %copy-done.4, f32[16,8,1792]{2,1,0:T(8,128)} %copy-done.5), custom_call_target="tpu_custom_call" | custom-call | flops 6000000000 | bytes 1000000 | tf_op jit(solution)/shard_map/final_map/pallas_call | solution.py:465
  (38 shorter events, 12.2 us)
Async XLA Ops:
  4.3 37.1 %copy-start.2 = (f32[4,8,2688]{2,1,0:T(8,128)S(1)}, f32[4,8,2688]{2,1,0:T(8,128)}, u32[]{:S(2)}) copy-start(f32[4,8,2688]{2,1,0:T(8,128)} %get-tuple-element.15) | copy-start | bytes 1032196
  4.3 4.2 %collective-permute-start.2 = (f32[3,8,512]{2,1,0:T(8,128)}, f32[3,8,512]{2,1,0:T(8,128)S(1)}, u32[]{:S(2)}, u32[]{:S(2)}) collective-permute-start(f32[3,8,512]{2,1,0:T(8,128)} %get-tuple-element.12.mine_ref), channel_id=1, source_target_pairs={{0,192},{64,128},{128,64},{192,0},{1,193},{65,129},{129,65},{193,1... | collective-permute-start | bytes 147464 | tf_op jit(solution)/shard_map/ppermute | solution.py:406
  5.9 4.0 %collective-permute-start.1 = (f32[3,8,512]{2,1,0:T(8,128)}, f32[3,8,512]{2,1,0:T(8,128)S(1)}, u32[]{:S(2)}, u32[]{:S(2)}) collective-permute-start(f32[3,8,512]{2,1,0:T(8,128)} %get-tuple-element.12.mine_ref), channel_id=1, source_target_pairs={{0,128},{64,192},{128,0},{192,64},{1,129},{65,193},{129,1},{193,65... | collective-permute-start | bytes 147464 | tf_op jit(solution)/shard_map/ppermute | solution.py:406
  7.3 4.4 %collective-permute-start = (f32[3,8,512]{2,1,0:T(8,128)}, f32[3,8,512]{2,1,0:T(8,128)S(1)}, u32[]{:S(2)}, u32[]{:S(2)}) collective-permute-start(f32[3,8,512]{2,1,0:T(8,128)} %get-tuple-element.12.mine_ref), channel_id=1, source_target_pairs={{0,64},{64,0},{128,192},{192,128},{1,65},{65,1},{129,193},{193,129... | collective-permute-start | bytes 147464 | tf_op jit(solution)/shard_map/ppermute | solution.py:406
  8.5 3.2 %copy-start.7 = (f32[3,8,512]{2,1,0:T(8,128)}, f32[3,8,512]{2,1,0:T(8,128)S(1)}, u32[]{:S(2)}) copy-start(f32[3,8,512]{2,1,0:T(8,128)S(1)} %collective-permute-done.2.across_ref) | copy-start | bytes 147460
  10.0 1.7 copy-start.8
  11.7 0.6 copy-start.9
  13.9 7.9 %collective-permute-start.3 = (f32[8,8,512]{2,1,0:T(8,128)}, f32[8,8,512]{2,1,0:T(8,128)S(1)}, u32[]{:S(2)}, u32[]{:S(2)}) collective-permute-start(f32[8,8,512]{2,1,0:T(8,128)} %combine_boxes.1), channel_id=1, source_target_pairs={{0,32},{1,33},{2,34},{3,35},{4,36},{5,37},{6,38},{7,39},{8,40},{9,... | collective-permute-start | bytes 393224 | tf_op jit(solution)/shard_map/ppermute | solution.py:371
  22.7 30.2 %copy-start.1 = (f32[8,8,512]{2,1,0:T(8,128)S(1)}, f32[8,8,512]{2,1,0:T(8,128)}, u32[]{:S(2)}) copy-start(f32[8,8,512]{2,1,0:T(8,128)} %combine_boxes.1) | copy-start | bytes 393220
  41.4 37.6 %copy-start = (f32[16,2,2,8,512]{4,3,2,1,0:T(8,128)}, f32[16,2,2,8,512]{4,3,2,1,0:T(8,128)S(1)}, u32[]{:S(2)}) copy-start(f32[16,2,2,8,512]{4,3,2,1,0:T(8,128)S(1)} %all_to_all.20.own_ref) | copy-start | bytes 3145732
  42.7 29.7 %all-to-all-start.2 = ((f32[16,8,2688]{2,1,0:T(8,128)}), f32[16,8,2688]{2,1,0:T(8,128)S(1)}, u32[]{:S(2)}, u32[]{:S(2)}) async-start(f32[16,8,2688]{2,1,0:T(8,128)} %bitcast.2), calls=%async_computation.2 | async-start | bytes 2752512 | tf_op jit(solution)/shard_map/all_to_all | solution.py:418
  74.4 5.4 %copy-start.3 = (f32[2,8,1792]{2,1,0:T(8,128)S(1)}, f32[2,8,1792]{2,1,0:T(8,128)}, u32[]{:S(2)}) copy-start(f32[2,8,1792]{2,1,0:T(8,128)} %get-tuple-element.18) | copy-start | bytes 344068
  74.4 52.0 %all-to-all-start.1 = ((f32[16,2,6,8,512]{4,3,2,1,0:T(8,128)}), f32[16,2,6,8,512]{4,3,2,1,0:T(8,128)}, u32[]{:S(2)}, u32[]{:S(2)}) async-start(f32[16,2,6,8,512]{4,3,2,1,0:T(8,128)} %broadcast_in_dim.16), calls=%async_computation.1 | async-start | bytes 6291456 | tf_op jit(solution)/shard_map/all_to_all | solution.py:376
  79.0 54.3 %collective-permute-start.4 = (f32[16,2,2,8,512]{4,3,2,1,0:T(8,128)S(1)}, f32[16,2,2,8,512]{4,3,2,1,0:T(8,128)}, u32[]{:S(2)}, u32[]{:S(2)}) collective-permute-start(f32[16,2,2,8,512]{4,3,2,1,0:T(8,128)S(1)} %all_to_all.20.own_ref), channel_id=1, source_target_pairs={{0,1},{1,0},{2,3},{3,2},{4,5},{5,4},{6,7},{7,6},{8,9},{9,8},{10,11... | collective-permute-start | bytes 3145736 | tf_op jit(solution)/shard_map/ppermute | solution.py:371
  79.8 8.7 %collective-permute-start.7 = (f32[2,8,1792]{2,1,0:T(8,128)S(1)}, f32[2,8,1792]{2,1,0:T(8,128)S(1)}, u32[]{:S(2)}, u32[]{:S(2)}) collective-permute-start(f32[2,8,1792]{2,1,0:T(8,128)S(1)} %copy-done.3), channel_id=1, source_target_pairs={{0,32},{1,33},{2,34},{3,35},{4,36},{5,37},{6,38},{7,39},{8,40},{9,... | collective-permute-start | bytes 344072 | tf_op jit(solution)/shard_map/ppermute | solution.py:371
  128.6 72.4 %all-to-all-start.3 = ((f32[16,2,2,8,1792]{4,3,2,1,0:T(8,128)}), f32[16,2,2,8,1792]{4,3,2,1,0:T(8,128)}, u32[]{:S(2)}, u32[]{:S(2)}) async-start(f32[16,2,2,8,1792]{4,3,2,1,0:T(8,128)} %broadcast_in_dim.18), calls=%async_computation.3 | async-start | bytes 7340032 | tf_op jit(solution)/shard_map/all_to_all | solution.py:376
  157.1 46.3 %collective-permute-start.5 = (f32[16,2,6,8,512]{4,3,2,1,0:T(8,128)}, f32[16,2,6,8,512]{4,3,2,1,0:T(8,128)}, u32[]{:S(2)}, u32[]{:S(2)}) collective-permute-start(f32[16,2,6,8,512]{4,3,2,1,0:T(8,128)} %all-to-all-done.1.own_ref), channel_id=1, source_target_pairs={{0,1},{1,0},{2,3},{3,2},{4,5},{5,4},{6,7},{7,6},{8,9},{9,8},{10,11... | collective-permute-start | bytes 9437192 | tf_op jit(solution)/shard_map/ppermute | solution.py:371
  158.7 44.7 %collective-permute-start.6 = (f32[16,8,896]{2,1,0:T(8,128)S(1)}, f32[16,8,896]{2,1,0:T(8,128)S(1)}, u32[]{:S(2)}, u32[]{:S(2)}) collective-permute-start(f32[16,8,896]{2,1,0:T(8,128)S(1)} %slice.16), channel_id=1, source_target_pairs={{0,0},{1,64},{2,128},{3,192},{4,4},{5,68},{6,132},{7,196},{8,8},{9... | collective-permute-start | bytes 1376264 | tf_op jit(solution)/shard_map/ppermute | solution.py:428
  163.4 88.1 %collective-permute-start.9 = (f32[16,8,1792]{2,1,0:T(8,128)S(1)}, f32[16,8,1792]{2,1,0:T(8,128)S(1)}, u32[]{:S(2)}, u32[]{:S(2)}) collective-permute-start(f32[16,8,1792]{2,1,0:T(8,128)S(1)} %slice.17), channel_id=1, source_target_pairs={{0,0},{4,4},{8,8},{12,12},{16,1},{20,5},{24,9},{28,13},{32,2},{36,... | collective-permute-start | bytes 2752520 | tf_op jit(solution)/shard_map/ppermute | solution.py:429
  201.0 50.5 %collective-permute-start.8 = (f32[16,2,2,8,1792]{4,3,2,1,0:T(8,128)}, f32[16,2,2,8,1792]{4,3,2,1,0:T(8,128)S(1)}, u32[]{:S(2)}, u32[]{:S(2)}) collective-permute-start(f32[16,2,2,8,1792]{4,3,2,1,0:T(8,128)} %all-to-all-done.3.own_ref), channel_id=1, source_target_pairs={{0,1},{1,0},{2,3},{3,2},{4,5},{5,4},{6,7},{7,6},{8,9},{9,8},{10,11... | collective-permute-start | bytes 11010056 | tf_op jit(solution)/shard_map/ppermute | solution.py:371
  203.4 0.8 copy-start.6
  251.5 1.0 copy-start.5
  251.5 2.1 copy-start.4
